TPU v7x, 32 devices: a whole 2x2x4 slice. The times are simulated.
32 devices in a mesh: groups: 2 (over y), feat: 4 (over z), layer: 2 (over x), row: 2 (over core).
Axes of the slice: x: 2, y: 2, z: 4, core: 2. Of those that a mesh axis runs over, the one named last changes fastest.
Arguments:
- resid_buf: bfloat16 [512, 2, 4608], P(('groups', 'feat', 'row')), parts along dimension 0, may hold values from -6 to 6
- shuffle: int32 [512], P('groups'), parts along dimension 0, may hold values from 0 to 255, each once
- mlp_out: bfloat16 [512, 2, 4608], P(('groups', 'feat', 'row')), parts along dimension 0, may hold values from -5 to 5
- enc_weight: bfloat16 [2, 8192, 4608], P('layer', 'feat', 'row'), may hold values from -0.09375 to 0.09375
- dec_weight: bfloat16 [2, 8192, 2, 4608], P('layer', 'feat', None, 'row'), may hold values from -0.0625 to 0.0625
- enc_bias: float32 [2, 8192], P('layer', 'feat'), may hold values from -0.5 to 0.5
- dec_bias: float32 [2, 4608], replicated, may hold values from -3 to 3
Outputs:
- rebuilt: bfloat16 [512, 2, 4608], P(('groups', 'feat', 'row')), parts along dimension 0
- enc_grad: bfloat16 [4, 8192, 4608], P(('groups', 'layer'), 'feat', 'row'), parts along dimension 0
- dec_grad: bfloat16 [4, 8192, 2, 4608], P(('groups', 'layer'), 'feat', None, 'row'), parts along dimension 0
- bias_grad: float32 [4, 8192], P(('groups', 'layer'), 'feat'), parts along dimension 0
There are 2 independent parts, one for each index of `groups`. A program takes and returns all parts, laid end to end along the dimension named above; an argument that names none is the same for every part. Nothing has to cross between parts.
Inputs may be any that keep to these rules, and one draw needn't show every extreme that they name: `shuffle`: a permutation of the 256 buffer rows.
All inputs are finite; a program needn't handle non-finite values.
Results may differ from a plain program's by a relative error of at most 0.04.
Values may be sent and summed in bfloat16 or wider, within the bound.
A program may use at most 128 MiB of HBM per device.

v0:
```python
import functools

import jax
import jax.numpy as jnp
from jax import lax
from jax.experimental import pallas as pl
from jax.experimental.pallas import tpu as pltpu
from jax.sharding import PartitionSpec as P

LAYERS = 2


def from_behind(block, axis, distance):
    devices = range(lax.axis_size(axis))
    route = [(i - distance, i) for i in devices if i - distance in devices]
    return lax.ppermute(block, axis, route)


def dot_last(left, right):
    return lax.dot_general(
        left, right, (((1,), (1,)), ((), ())), preferred_element_type=jnp.float32
    )


def dot_first(left, right):
    return lax.dot_general(
        left, right, (((0,), (0,)), ((), ())), preferred_element_type=jnp.float32
    )


def on_device(resid_buf, shuffle, mlp_out, enc_weight, dec_weight, enc_bias, dec_bias):
    feat_count = lax.axis_size("feat")
    row_count = lax.axis_size("row")
    sub_blocks = lax.axis_size("layer") // LAYERS
    layer_pos = lax.axis_index("layer")
    row_pos = lax.axis_index("row")
    source = layer_pos // sub_blocks
    rows_each = resid_buf.shape[0]
    width = dec_bias.shape[1]
    half_width = enc_weight.shape[2]
    local_rows = rows_each * feat_count
    total_rows = local_rows * row_count
    loss_scale = float(total_rows) ** (-0.5)
    own_layer = lax.dynamic_index_in_dim(resid_buf, source, axis=1, keepdims=False)
    buffer_all = lax.all_gather(own_layer, ("feat", "row"), axis=0, tiled=True)
    batch_rows = jnp.take(buffer_all, shuffle, axis=0)
    blocks = batch_rows.reshape(feat_count, row_count, rows_each, width)
    inputs_half = lax.dynamic_slice_in_dim(
        jnp.swapaxes(blocks, 0, 1), row_pos * half_width, half_width, axis=3
    )
    inputs_half = inputs_half.reshape(total_rows, half_width)
    own_half_dec = dec_weight[0][:, 0]
    next_half_dec = dec_weight[0][:, 1]
    pre_all = lax.psum(dot_last(inputs_half, enc_weight[0]), "row") + enc_bias[0]
    features_all = jnp.maximum(pre_all, 0.0).astype(jnp.bfloat16)
    own_part = jnp.dot(features_all, own_half_dec, preferred_element_type=jnp.float32)
    next_part = jnp.dot(features_all, next_half_dec, preferred_element_type=jnp.float32)
    carried = from_behind(next_part, "layer", sub_blocks)
    spread = (own_part + carried).reshape(row_count, local_rows, half_width)
    halves = lax.psum_scatter(spread, "feat", scatter_dimension=1, tiled=True)
    joined = lax.all_to_all(halves, "row", split_axis=0, concat_axis=2, tiled=True)
    section_sum = joined.reshape(rows_each, width)
    target_ids = jnp.arange(LAYERS, dtype=jnp.int32)
    target_slots = jnp.where((target_ids == source)[:, None, None], section_sum[None], 0.0)
    totals = lax.psum(target_slots, "layer")
    recon_sum = jnp.swapaxes(totals, 0, 1) + dec_bias[None]
    errors = (recon_sum - mlp_out.astype(jnp.float32)).astype(jnp.bfloat16)
    gathered = lax.all_gather(errors, ("feat", "row"), axis=0, tiled=True)
    error_grid = gathered.reshape(feat_count, row_count, rows_each, LAYERS, width)
    errors_mine = lax.dynamic_index_in_dim(error_grid, row_pos, axis=1, keepdims=False)
    errors_mine = errors_mine.reshape(local_rows, LAYERS, width)
    errors_half = lax.dynamic_slice_in_dim(
        jnp.swapaxes(error_grid, 0, 1), row_pos * half_width, half_width, axis=4
    )
    errors_half = errors_half.reshape(total_rows, LAYERS, half_width)
    live_next = source + 1 < LAYERS
    next_index = jnp.minimum(source + 1, LAYERS - 1)
    half_own = lax.dynamic_index_in_dim(errors_half, source, axis=1, keepdims=False)
    half_next = lax.dynamic_index_in_dim(errors_half, next_index, axis=1, keepdims=False)
    half_next = jnp.where(live_next, half_next, jnp.zeros_like(half_next))
    half_terms = dot_last(half_own, own_half_dec) + dot_last(half_next, next_half_dec)
    grad_feats = lax.psum(half_terms, "row") * loss_scale
    grad_all = jnp.where(pre_all > 0, grad_feats, 0.0).astype(jnp.bfloat16)
    grad_own = loss_scale * dot_first(features_all, half_own)
    grad_next = loss_scale * dot_first(features_all, half_next)
    enc_grad = dot_first(grad_all, inputs_half).astype(jnp.bfloat16)
    dec_grad = jnp.stack([grad_own, grad_next], axis=1).astype(jnp.bfloat16)
    bias_grad = jnp.sum(grad_all.astype(jnp.float32), axis=0)
    return (recon_sum.astype(jnp.bfloat16), enc_grad[None], dec_grad[None], bias_grad[None])

KC = 256
DC = 128
MESH = pl.DeviceIdType.MESH
VMEM_LIMIT = 67043328
BF = jnp.bfloat16


def pick(rows, cols, stride, offset):
    r = lax.broadcasted_iota(jnp.int32, (rows, cols), 0)
    c = lax.broadcasted_iota(jnp.int32, (rows, cols), 1)
    return (c == stride * r + offset).astype(BF)


def mm(left, right):
    return jnp.dot(left, right, preferred_element_type=jnp.float32)


def step_kernel(
    n, J, res, shuf, mlp, enc, dec, bias, dbias,
    feats, xs, errs, gpre, parts,
    enc_v, wv, raw, xsend, xg, mlpx, msend, pre_own, pre_send, pre_recv, fall,
    nsend, nrecv, facc, osend, rrecv, e0, e1, rc, rb, g_own, g_send, g_recv, gall,
    sem_l, sem_raw, x_s, x_r, m_s, m_r, p_s, p_r, f_s, f_r, n_s, n_r, r_s, r_r,
    e_s, e_r, t_s, t_r, b_s, b_r, g_s, g_r, q_s, q_r, y_s, w_s,
):
    z = lax.axis_index("feat")
    x = lax.axis_index("layer")
    c = lax.axis_index("row")
    R, H = xsend.shape[1:]
    F = enc_v.shape[0]
    T = xs.shape[0]
    T2, CR, NC = T // 2, 2 * R, H // J
    nk = F // KC
    scale = float(T) ** (-0.5)
    other_c, other_x = 1 - c, 1 - x

    def far(dz):
        return lax.rem(z + dz, n)

    def back(dz):
        return lax.rem(z + n - dz, n)

    def remote(src, dst, send, recv, **where):
        return pltpu.make_async_remote_copy(
            src_ref=src, dst_ref=dst, send_sem=send, recv_sem=recv,
            device_id=where, device_id_type=MESH)

    line = n == 4

    def unless_ends(dz, act):
        if line and dz == n - 1:
            pl.when(z != 0)(act)
        elif line and dz == 1:
            pl.when(z != n - 1)(act)
        else:
            act()

    def relays(act):
        if line:
            pl.when(z == 2)(lambda: act(1, 3))
            pl.when(z == 1)(lambda: act(3, 1))

    orders = (2, 1, 3) if line else tuple(range(1, n))

    enc_copy = pltpu.make_async_copy(enc, enc_v, sem_l)
    enc_copy.start()

    def raw_copy(i, slot):
        return pltpu.make_async_copy(
            dec.reshape(2 * F, H).at[pl.ds(pl.multiple_of(i * 2 * DC, 2 * DC), 2 * DC)], raw.at[slot], sem_raw.at[slot])

    raw_copy(0, 0).start()

    barrier = pltpu.get_barrier_semaphore()
    for dz in range(n):
        if dz:
            pl.semaphore_signal(barrier, inc=1, device_id={"feat": far(dz), "row": c}, device_id_type=MESH)
        pl.semaphore_signal(barrier, inc=1, device_id={"feat": far(dz), "row": other_c}, device_id_type=MESH)
    for cc in (c, other_c):
        pl.semaphore_signal(barrier, inc=1, device_id={"layer": other_x, "row": cc}, device_id_type=MESH)

    own_x = mm(pick(R, 2 * R, 2, x), res.reshape(2 * R, 2 * H)[...]).astype(BF)
    x_mine = jnp.where(c == 0, own_x[:, :H], own_x[:, H:])
    xsend[0] = x_mine
    xsend[1] = jnp.where(c == 0, own_x[:, H:], own_x[:, :H])
    xg[z, c] = x_mine
    own_m = mm(pick(R, 2 * R, 2, x), mlp.reshape(2 * R, 2 * H)[...]).astype(BF)
    mlpx[c] = jnp.where(c == 0, own_m[:, :H], own_m[:, H:])
    msend[...] = jnp.where(c == 0, own_m[:, H:], own_m[:, :H])

    pl.semaphore_wait(barrier, 2 * n + 1)

    def x_copy(dz, k):
        return remote(xsend.at[k], xg.at[z, c], x_s.at[dz, k], x_r.at[dz, k],
                      feat=far(dz), row=c if k == 0 else other_c)

    x_list = [(dz, k) for dz in orders for k in range(2)] + [(0, 1)]
    for dz, k in x_list:
        unless_ends(dz, lambda: x_copy(dz, k).start())

    def y_copy(k, to, at):
        cc = c if k == 0 else other_c
        return remote(xg.at[back(2), cc], xg.at[back(2), cc], y_s.at[k], x_r.at[at, k], feat=far(to))

    m_copy = remote(msend, mlpx.at[c], m_s, m_r, row=other_c)
    m_copy.start()

    apart = jnp.concatenate([pick(DC, 2 * DC, 2, 0), pick(DC, 2 * DC, 2, 1)], axis=0)
    nd = F // DC

    def split_body(i, carry):
        slot = lax.rem(i, 2)

        @pl.when(i + 1 < nd)
        def _():
            raw_copy(i + 1, 1 - slot).start()

        raw_copy(i, slot).wait()
        both = mm(apart, raw[slot]).astype(BF)
        rows = pl.ds(pl.multiple_of(i * DC, DC), DC)
        wv[0, rows, :] = both[:DC]
        wv[1, rows, :] = both[DC:]
        return carry

    lax.fori_loop(0, nd // 2, split_body, 0)
    if line:
        for k in range(2):
            x_copy(2, k).wait_recv()
            relays(lambda to, at: y_copy(k, to, at).start())
    lax.fori_loop(nd // 2, nd, split_body, 0)

    for dz, k in x_list:
        if not line or dz != 2:
            x_copy(dz, k).wait_recv()
    perm = (lax.broadcasted_iota(jnp.int32, (T, T), 0) == shuf[...]).astype(BF)

    def perm_body(q, carry):
        cols = pl.ds(pl.multiple_of(q * KC, KC), KC)
        xs[:, cols] = dot_first(perm, xg[:, :, :, cols].reshape(T, KC)).astype(BF)
        return carry

    lax.fori_loop(0, H // KC, perm_body, 0)
    enc_copy.wait()

    def cols_of(k):
        return pl.ds(pl.multiple_of(k * KC, KC), KC)

    def keep_and_send(v, k, own, send):
        top, bot = v[:T2], v[T2:]
        own[k] = jnp.where(c == 0, top, bot)
        send[k] = jnp.where(c == 0, bot, top)

    def p_copy(k):
        return remote(pre_send.at[k], pre_recv.at[k], p_s.at[k], p_r.at[k], row=other_c)

    def f_copy(k):
        return remote(fall.at[c, k], fall.at[c, k], f_s.at[k], f_r.at[k], row=other_c)

    def pre_body(k, carry):
        keep_and_send(dot_last(xs[...], enc_v[cols_of(k), :]), k, pre_own, pre_send)
        p_copy(k).start()
        return carry

    lax.fori_loop(0, nk, pre_body, 0)

    def feat_body(k, carry):
        p_copy(k).wait_recv()
        v = pre_own[k] + pre_recv[k] + bias[:, cols_of(k)]
        fall[c, k] = jnp.maximum(v, 0.0).astype(BF)
        f_copy(k).start()
        return carry

    lax.fori_loop(0, nk, feat_body, 0)

    def join_body(k, carry):
        f_copy(k).wait_recv()
        feats[:, cols_of(k)] = jnp.concatenate([fall[0, k], fall[1, k]], axis=0)
        return carry

    lax.fori_loop(0, nk, join_body, 0)

    def n_copy(j):
        return remote(nsend.at[j], nrecv.at[j], n_s.at[j], n_r.at[j], layer=other_x)

    def r_copy(j, dz):
        return remote(osend.at[j, far(dz)], rrecv.at[j, dz - 1], r_s.at[j, dz], r_r.at[j, dz], feat=far(dz))

    def e_copy(j, dz):
        return remote(e0.at[j, z], e0.at[j, z], e_s.at[j, dz], e_r.at[j, dz], feat=far(dz))

    def w_copy(j, to, at):
        return remote(e0.at[j, back(2)], e0.at[j, back(2)], w_s.at[j], e_r.at[j, at], feat=far(to))

    def t_copy(j, dz):
        return remote(e0.at[j, back(dz)], e1.at[j, back(dz)], t_s.at[j, dz], t_r.at[j, dz], layer=other_x)

    def spots(j, q):
        wide = pl.ds(pl.multiple_of(j * NC + q * KC, KC), KC)
        return wide, pl.ds(pl.multiple_of(q * KC, KC), KC)

    @pl.when(x == 0)
    def _():
        for j in range(J):
            def next_body(q, carry):
                wide, near = spots(j, q)
                nsend[j, :, near] = mm(feats[...], wv[1, :, wide]).astype(BF)
                return carry

            lax.fori_loop(0, NC // KC, next_body, 0)
            n_copy(j).start()

            def own_body(q, carry):
                wide, near = spots(j, q)
                v = mm(feats[...], wv[0, :, wide]).reshape(n, CR, KC)
                facc[:, :, wide] = v
                osend[j, :, :, near] = v.astype(BF)
                return carry

            lax.fori_loop(0, NC // KC, own_body, 0)
            for dz in range(1, n):
                r_copy(j, dz).start()

    @pl.when(x == 1)
    def _():
        for j in range(J):
            def own_body(q, carry):
                wide, near = spots(j, q)
                facc[:, :, wide] = mm(feats[...], wv[0, :, wide]).reshape(n, CR, KC)
                return carry

            lax.fori_loop(0, NC // KC, own_body, 0)
        for j in range(J):
            n_copy(j).wait_recv()

            def add_body(q, carry):
                wide, near = spots(j, q)
                v = facc[:, :, wide] + nrecv[j, :, near].astype(jnp.float32).reshape(n, CR, KC)
                facc[:, :, wide] = v
                osend[j, :, :, near] = v.astype(BF)
                return carry

            lax.fori_loop(0, NC // KC, add_body, 0)
            for dz in range(1, n):
                r_copy(j, dz).start()

    m_copy.wait_recv()

    def reduce_chunk(j):
        for dz in range(1, n):
            r_copy(j, dz).wait_recv()
        wide = pl.ds(j * NC, NC)
        total = facc[z, :, wide]
        for dz in range(1, n):
            total = total + rrecv[j, dz - 1].astype(jnp.float32)
        d = jnp.where(
            x == 0,
            jnp.where(c == 0, dbias[0:1, j * NC:(j + 1) * NC], dbias[0:1, H + j * NC:H + (j + 1) * NC]),
            jnp.where(c == 0, dbias[1:2, j * NC:(j + 1) * NC], dbias[1:2, H + j * NC:H + (j + 1) * NC]))
        total = total + d
        e0[j, z] = (total - mlpx[:, :, wide].reshape(CR, NC).astype(jnp.float32)).astype(BF)
        for dz in orders:
            unless_ends(dz, lambda: e_copy(j, dz).start())

        @pl.when(x == 1)
        def _():
            t_copy(j, 0).start()

        rc[:, j] = total.astype(BF).reshape(2, R, NC)

    def pass_chunk(j):
        for dz in orders:
            e_copy(j, dz).wait_recv()
            if line and dz == 2:
                relays(lambda to, at: w_copy(j, to, at).start())

            @pl.when(x == 1)
            def _():
                t_copy(j, dz).start()

    for j in range(J):
        reduce_chunk(j)
        if j:
            pass_chunk(j - 1)
    pass_chunk(J - 1)

    def b_copy(k):
        dx, dc = k // 2, k % 2
        to_x = other_x if dx else x
        to_c = other_c if dc else c
        return remote(rc.at[to_c], rb.at[x, c], b_s.at[k], b_r.at[k], layer=to_x, row=to_c)

    for k in range(1, 4):
        b_copy(k).start()
    rb[x, c] = rc[c]

    for j in range(J):
        errs[0, :, j * NC:(j + 1) * NC] = e0[j].reshape(T, NC)

    @pl.when(x == 0)
    def _():
        for j in range(J):
            for dz in range(n):
                t_copy(j, dz).wait_recv()
            errs[1, :, j * NC:(j + 1) * NC] = e1[j].reshape(T, NC)

    @pl.when(x == 1)
    def _():
        errs[1] = jnp.zeros((T, H), BF)

    def g_copy(k):
        return remote(g_send.at[k], g_recv.at[k], g_s.at[k], g_r.at[k], row=other_c)

    def q_copy(k):
        return remote(gall.at[c, k], gall.at[c, k], q_s.at[k], q_r.at[k], row=other_c)

    @pl.when(x == 0)
    def _():
        def grad_body(k, carry):
            v = dot_last(errs[0], wv[0, cols_of(k), :]) + dot_last(errs[1], wv[1, cols_of(k), :])
            keep_and_send(v, k, g_own, g_send)
            g_copy(k).start()
            return carry

        lax.fori_loop(0, nk, grad_body, 0)

    @pl.when(x == 1)
    def _():
        def grad_body(k, carry):
            keep_and_send(dot_last(errs[0], wv[0, cols_of(k), :]), k, g_own, g_send)
            g_copy(k).start()
            return carry

        lax.fori_loop(0, nk, grad_body, 0)

    def mask_body(k, carry):
        g_copy(k).wait_recv()
        v = (g_own[k] + g_recv[k]) * scale
        gall[c, k] = jnp.where(fall[c, k].astype(jnp.float32) > 0, v, 0.0).astype(BF)
        q_copy(k).start()
        return carry

    lax.fori_loop(0, nk, mask_body, 0)

    for k in range(1, 4):
        b_copy(k).wait_recv()
    for h in range(2):
        for j in range(J):
            lo = h * H + j * NC
            parts[:, lo:lo + NC] = rb[:, h, j].reshape(2 * R, NC)

    def last_body(k, carry):
        q_copy(k).wait_recv()
        both = jnp.concatenate([gall[0, k], gall[1, k]], axis=0)
        gpre[:, cols_of(k)] = both
        p_copy(k).wait_send()
        f_copy(k).wait_send()
        g_copy(k).wait_send()
        q_copy(k).wait_send()
        return carry

    lax.fori_loop(0, nk, last_body, 0)

    for dz, k in x_list:
        unless_ends(dz, lambda: x_copy(dz, k).wait_send())
    for k in range(2):
        relays(lambda to, at: y_copy(k, to, at).wait_send())
    for j in range(J):
        relays(lambda to, at: w_copy(j, to, at).wait_send())
    m_copy.wait_send()
    for j in range(J):
        for dz in range(1, n):
            r_copy(j, dz).wait_send()
            unless_ends(dz, lambda: e_copy(j, dz).wait_send())
    for k in range(1, 4):
        b_copy(k).wait_send()

    @pl.when(x == 0)
    def _():
        for j in range(J):
            n_copy(j).wait_send()

    @pl.when(x == 1)
    def _():
        for j in range(J):
            for dz in range(n):
                t_copy(j, dz).wait_send()


def weight_kernel(scale, feats, gpre, errs, xs, parts, enc_grad, dec_grad, bgrad, rebuilt):
    fc, H = enc_grad.shape
    R2 = parts.shape[0]

    @pl.when(pl.program_id(0) == 0)
    def _():
        i = lax.broadcasted_iota(jnp.int32, (R2, R2), 0)
        j = lax.broadcasted_iota(jnp.int32, (R2, R2), 1)
        inter = (j == (i % 2) * (R2 // 2) + i // 2).astype(BF)
        rebuilt.reshape(R2, 2 * H)[...] = mm(inter, parts[...]).astype(BF)

    bgrad[...] = jnp.sum(gpre[...].astype(jnp.float32), axis=0, keepdims=True)
    enc_grad[...] = dot_first(gpre[...], xs[...]).astype(BF)
    p0, p1 = pick(DC, 2 * DC, 2, 0), pick(DC, 2 * DC, 2, 1)
    out = dec_grad.reshape(2 * fc, H)
    for b in range(fc // DC):
        f = feats[:, b * DC:(b + 1) * DC]
        g = dot_first(mm(f, p0).astype(BF), errs[0]) + dot_first(mm(f, p1).astype(BF), errs[1])
        out[b * 2 * DC:(b + 1) * 2 * DC, :] = (scale * g).astype(BF)


def fused(resid_buf, shuffle, mlp_out, enc_weight, dec_weight, enc_bias, dec_bias):
    n = lax.axis_size("feat")
    R = resid_buf.shape[0]
    F, H = enc_weight.shape[1:]
    T = R * n * 2
    T2, CR = T // 2, 2 * R
    J = H // KC
    NC, nk = H // J, F // KC
    f32 = jnp.float32
    vm = pl.BlockSpec(memory_space=pltpu.VMEM)
    hbm = pl.BlockSpec(memory_space=pl.ANY)
    dma = pltpu.SemaphoreType.DMA
    shape = jax.ShapeDtypeStruct
    feats, xs, errs, gpre, parts = pl.pallas_call(
        functools.partial(step_kernel, n, J),
        out_shape=(
            shape((T, F), BF), shape((T, H), BF), shape((2, T, H), BF), shape((T, F), BF),
            shape((2 * R, 2 * H), BF)),
        in_specs=[vm, vm, vm, hbm, hbm, vm, vm],
        out_specs=[vm] * 5,
        scratch_shapes=[
            pltpu.VMEM((F, H), BF), pltpu.VMEM((2, F, H), BF), pltpu.VMEM((2, 2 * DC, H), BF),
            pltpu.VMEM((2, R, H), BF), pltpu.VMEM((n, 2, R, H), BF),
            pltpu.VMEM((2, R, H), BF), pltpu.VMEM((R, H), BF),
            pltpu.VMEM((nk, T2, KC), f32), pltpu.VMEM((nk, T2, KC), f32), pltpu.VMEM((nk, T2, KC), f32),
            pltpu.VMEM((2, nk, T2, KC), BF),
            pltpu.VMEM((J, T, NC), BF), pltpu.VMEM((J, T, NC), BF), pltpu.VMEM((n, CR, H), f32),
            pltpu.VMEM((J, n, CR, NC), BF), pltpu.VMEM((J, n - 1, CR, NC), BF),
            pltpu.VMEM((J, n, CR, NC), BF), pltpu.VMEM((J, n, CR, NC), BF),
            pltpu.VMEM((2, J, R, NC), BF), pltpu.VMEM((2, 2, J, R, NC), BF),
            pltpu.VMEM((nk, T2, KC), f32), pltpu.VMEM((nk, T2, KC), f32), pltpu.VMEM((nk, T2, KC), f32),
            pltpu.VMEM((2, nk, T2, KC), BF),
            dma, dma((2,)), dma((n, 2)), dma((n, 2)), dma, dma, dma((nk,)), dma((nk,)),
            dma((nk,)), dma((nk,)), dma((J,)), dma((J,)), dma((J, n)), dma((J, n)),
            dma((J, n)), dma((J, n)), dma((J, n)), dma((J, n)), dma((4,)), dma((4,)),
            dma((nk,)), dma((nk,)), dma((nk,)), dma((nk,)), dma((2,)), dma((J,)),
        ],
        compiler_params=pltpu.CompilerParams(
            collective_id=0, has_side_effects=True, vmem_limit_bytes=VMEM_LIMIT),
    )(resid_buf, shuffle.reshape(1, T), mlp_out, enc_weight[0], dec_weight[0], enc_bias, dec_bias)
    fc = 512 if F % 512 == 0 else KC
    enc_grad, dec_grad, bgrad, rebuilt = pl.pallas_call(
        functools.partial(weight_kernel, float(T) ** (-0.5)),
        grid=(F // fc,),
        out_shape=(
            shape((F, H), BF), shape((F, 2, H), BF), shape((1, F), f32), shape((R, 2, 2 * H), BF)),
        in_specs=[
            pl.BlockSpec((T, fc), lambda i: (0, i)), pl.BlockSpec((T, fc), lambda i: (0, i)),
            pl.BlockSpec((2, T, H), lambda i: (0, 0, 0)), pl.BlockSpec((T, H), lambda i: (0, 0)),
            pl.BlockSpec((2 * R, 2 * H), lambda i: (0, 0))],
        out_specs=(
            pl.BlockSpec((fc, H), lambda i: (i, 0)), pl.BlockSpec((fc, 2, H), lambda i: (i, 0, 0)),
            pl.BlockSpec((1, fc), lambda i: (0, i)), pl.BlockSpec((R, 2, 2 * H), lambda i: (0, 0, 0))),
        compiler_params=pltpu.CompilerParams(vmem_limit_bytes=VMEM_LIMIT),
    )(feats, gpre, errs, xs, parts)
    return rebuilt, enc_grad[None], dec_grad[None], bgrad


def chosen(resid_buf, shuffle, mlp_out, enc_weight, dec_weight, enc_bias, dec_bias):
    args = (resid_buf, shuffle, mlp_out, enc_weight, dec_weight, enc_bias, dec_bias)
    rows, width = resid_buf.shape[0], enc_weight.shape[2]
    fits = (
        lax.axis_size("layer") == LAYERS == 2 and lax.axis_size("row") == 2
        and 1 < lax.axis_size("feat") <= 4 and rows % 16 == 0
        and width % KC == 0 and enc_weight.shape[1] % KC == 0)
    return fused(*args) if fits else on_device(*args)


def solution(mesh):
    return jax.shard_map(
        chosen,
        mesh=mesh,
        in_specs=(
            P(("groups", "feat", "row"), None, None),
            P("groups"),
            P(("groups", "feat", "row"), None, None),
            P("layer", "feat", "row"),
            P("layer", "feat", None, "row"),
            P("layer", "feat"),
            P(),
        ),
        out_specs=(
            P(("groups", "feat", "row"), None, None),
            P(("groups", "layer"), "feat", "row"),
            P(("groups", "layer"), "feat", None, "row"),
            P(("groups", "layer"), "feat"),
        ),
        check_vma=False,
    )
```

profile of v0, /device:TPU:0, one launch (start us, length us, event | category | flops | bytes accessed | tf_op | source)
XLA Modules:
  0.0 140.5 jit_solution(17272379841914600845)
XLA Ops:
  0.6 117.1 %shard_map.102 = (bf16[256,2048]{1,0:T(8,128)(2,1)}, bf16[256,2304]{1,0:T(8,128)(2,1)}, bf16[2,256,2304]{2,1,0:T(8,128)(2,1)}, bf16[256,2048]{1,0:T(8,128)(2,1)}, bf16[64,4608]{1,0:T(8,128)(2,1)}) custom-call(bf16[32,2,4608]{2,1,0:T(2,128)(2,1)} %res.1, s32[1,256]{1,0:T(1,128)} %bitcast.7, bf16[32,2,4608]{2,1,0:T(2,128)(2,1)} %mlp.1, ...), custom_call_target="tpu_custom_call" | custom-call | tf_op jit(solution)/shard_map/pallas_call | solution.py:513
  117.7 22.7 %shard_map.103 = (bf16[2048,2304]{1,0:T(8,128)(2,1)}, bf16[2048,2,2304]{2,1,0:T(2,128)(2,1)}, f32[1,2048]{1,0:T(1,128)}, bf16[32,2,4608]{2,1,0:T(2,128)(2,1)}) custom-call(bf16[256,2048]{1,0:T(8,128)(2,1)} %get-tuple-element.13.feats, bf16[256,2048]{1,0:T(8,128)(2,1)} %get-tuple-element.14.gpre, bf16[2,256,2304]{2,1,0:T(8,128)(2,1)} %get-tuple-element.15.errs, ...), custom_call_target="tpu_custom_call" | custom-call | tf_op jit(solution)/shard_map/pallas_call | solution.py:541
where the time goes:
time: 141 us; the launch traced here: 140 us
  Pallas kernels  140 us (99%)
    pallas_call x1, Pallas kernels, fused(): pl.pallas_call(functools.partial(step_kernel, n, J), out_shape=(shape((T,...  117 us
    pallas_call x1, Pallas kernels, fused(): pl.pallas_call(functools.partial(weight_kernel, float(T) ** (-0.5)), grid...  22.7 us

commit v1 on v0

--- a/solution.py
+++ b/solution.py
@@ -101,14 +101,20 @@
     return (c == stride * r + offset).astype(BF)
 
 
+def spread_to(offset):
+    r = lax.broadcasted_iota(jnp.int32, (2 * DC, DC), 0)
+    c = lax.broadcasted_iota(jnp.int32, (2 * DC, DC), 1)
+    return (r == 2 * c + offset).astype(BF)
+
+
 def mm(left, right):
     return jnp.dot(left, right, preferred_element_type=jnp.float32)
 
 
 def step_kernel(
     n, J, res, shuf, mlp, enc, dec, bias, dbias,
-    feats, xs, errs, gpre, parts,
-    enc_v, wv, raw, xsend, xg, mlpx, msend, pre_own, pre_send, pre_recv, fall,
+    fx, xs, errs, gpre, parts,
+    feats, enc_v, wv, raw, xsend, xg, mlpx, msend, pre_own, pre_send, pre_recv, fall,
     nsend, nrecv, facc, osend, rrecv, e0, e1, rc, rb, g_own, g_send, g_recv, gall,
     sem_l, sem_raw, x_s, x_r, m_s, m_r, p_s, p_r, f_s, f_r, n_s, n_r, r_s, r_r,
     e_s, e_r, t_s, t_r, b_s, b_r, g_s, g_r, q_s, q_r, y_s, w_s,
@@ -269,6 +275,15 @@
 
     lax.fori_loop(0, nk, join_body, 0)
 
+    up0, up1 = spread_to(0), spread_to(1)
+
+    def expand_body(b, carry):
+        rows = pl.ds(pl.multiple_of(b * 2 * DC, 2 * DC), 2 * DC)
+        turned = feats[:, pl.ds(pl.multiple_of(b * DC, DC), DC)].T
+        fx[rows, :T] = mm(up0, turned).astype(BF)
+        fx[rows, T:] = mm(up1, turned).astype(BF)
+        return carry
+
     def n_copy(j):
         return remote(nsend.at[j], nrecv.at[j], n_s.at[j], n_r.at[j], layer=other_x)
 
@@ -333,6 +348,7 @@
             for dz in range(1, n):
                 r_copy(j, dz).start()
 
+    lax.fori_loop(0, F // DC, expand_body, 0)
     m_copy.wait_recv()
 
     def reduce_chunk(j):
@@ -476,25 +492,54 @@
                 t_copy(j, dz).wait_send()
 
 
-def weight_kernel(scale, feats, gpre, errs, xs, parts, enc_grad, dec_grad, bgrad, rebuilt):
-    fc, H = enc_grad.shape
+def weight_kernel(scale, fx, gpre, errs, xs, parts, enc_grad, dec_grad, bgrad, rebuilt, dbuf, ebuf, dsem, esem):
+    T, F = gpre.shape
+    H = xs.shape[1]
     R2 = parts.shape[0]
-
-    @pl.when(pl.program_id(0) == 0)
-    def _():
-        i = lax.broadcasted_iota(jnp.int32, (R2, R2), 0)
-        j = lax.broadcasted_iota(jnp.int32, (R2, R2), 1)
-        inter = (j == (i % 2) * (R2 // 2) + i // 2).astype(BF)
-        rebuilt.reshape(R2, 2 * H)[...] = mm(inter, parts[...]).astype(BF)
-
+    x = lax.axis_index("layer")
+    nb = F // KC
+
+    def d_copy(i, slot):
+        rows = pl.ds(pl.multiple_of(i * 2 * KC, 2 * KC), 2 * KC)
+        return pltpu.make_async_copy(dbuf.at[slot], dec_grad.reshape(2 * F, H).at[rows], dsem.at[slot])
+
+    def e_copy(i, slot):
+        rows = pl.ds(pl.multiple_of(i * KC, KC), KC)
+        return pltpu.make_async_copy(ebuf.at[slot], enc_grad.at[rows], esem.at[slot])
+
+    def block(i, carry):
+        slot = lax.rem(i, 2)
+
+        @pl.when(i >= 2)
+        def _():
+            d_copy(i - 2, slot).wait()
+            e_copy(i - 2, slot).wait()
+
+        rows = pl.ds(pl.multiple_of(i * 2 * KC, 2 * KC), 2 * KC)
+
+        @pl.when(x == 0)
+        def _():
+            dbuf[slot] = (scale * mm(fx[rows, :], errs.reshape(2 * T, H)[...])).astype(BF)
+
+        @pl.when(x == 1)
+        def _():
+            dbuf[slot] = (scale * mm(fx[rows, :T], errs[0])).astype(BF)
+
+        d_copy(i, slot).start()
+        cols = pl.ds(pl.multiple_of(i * KC, KC), KC)
+        ebuf[slot] = dot_first(gpre[:, cols], xs[...]).astype(BF)
+        e_copy(i, slot).start()
+        return carry
+
+    lax.fori_loop(0, nb, block, 0)
     bgrad[...] = jnp.sum(gpre[...].astype(jnp.float32), axis=0, keepdims=True)
-    enc_grad[...] = dot_first(gpre[...], xs[...]).astype(BF)
-    p0, p1 = pick(DC, 2 * DC, 2, 0), pick(DC, 2 * DC, 2, 1)
-    out = dec_grad.reshape(2 * fc, H)
-    for b in range(fc // DC):
-        f = feats[:, b * DC:(b + 1) * DC]
-        g = dot_first(mm(f, p0).astype(BF), errs[0]) + dot_first(mm(f, p1).astype(BF), errs[1])
-        out[b * 2 * DC:(b + 1) * 2 * DC, :] = (scale * g).astype(BF)
+    i = lax.broadcasted_iota(jnp.int32, (R2, R2), 0)
+    j = lax.broadcasted_iota(jnp.int32, (R2, R2), 1)
+    inter = (j == (i % 2) * (R2 // 2) + i // 2).astype(BF)
+    rebuilt.reshape(R2, 2 * H)[...] = mm(inter, parts[...]).astype(BF)
+    for k in range(max(nb - 2, 0), nb):
+        d_copy(k, k % 2).wait()
+        e_copy(k, k % 2).wait()
 
 
 def fused(resid_buf, shuffle, mlp_out, enc_weight, dec_weight, enc_bias, dec_bias):
@@ -510,15 +555,15 @@
     hbm = pl.BlockSpec(memory_space=pl.ANY)
     dma = pltpu.SemaphoreType.DMA
     shape = jax.ShapeDtypeStruct
-    feats, xs, errs, gpre, parts = pl.pallas_call(
+    outs = ((2 * F, 2 * T), (T, H), (2, T, H), (T, F), (2 * R, 2 * H))
+    held = sum(2 * a[-1] * (a[0] * a[1] if len(a) == 3 else a[0]) for a in outs)
+    fx, xs, errs, gpre, parts = pl.pallas_call(
         functools.partial(step_kernel, n, J),
-        out_shape=(
-            shape((T, F), BF), shape((T, H), BF), shape((2, T, H), BF), shape((T, F), BF),
-            shape((2 * R, 2 * H), BF)),
+        out_shape=tuple(pltpu.VMEM(a, BF) for a in outs),
         in_specs=[vm, vm, vm, hbm, hbm, vm, vm],
-        out_specs=[vm] * 5,
+        out_specs=(vm,) * 5,
         scratch_shapes=[
-            pltpu.VMEM((F, H), BF), pltpu.VMEM((2, F, H), BF), pltpu.VMEM((2, 2 * DC, H), BF),
+            pltpu.VMEM((T, F), BF), pltpu.VMEM((F, H), BF), pltpu.VMEM((2, F, H), BF), pltpu.VMEM((2, 2 * DC, H), BF),
             pltpu.VMEM((2, R, H), BF), pltpu.VMEM((n, 2, R, H), BF),
             pltpu.VMEM((2, R, H), BF), pltpu.VMEM((R, H), BF),
             pltpu.VMEM((nk, T2, KC), f32), pltpu.VMEM((nk, T2, KC), f32), pltpu.VMEM((nk, T2, KC), f32),
@@ -535,23 +580,18 @@
             dma((nk,)), dma((nk,)), dma((nk,)), dma((nk,)), dma((2,)), dma((J,)),
         ],
         compiler_params=pltpu.CompilerParams(
-            collective_id=0, has_side_effects=True, vmem_limit_bytes=VMEM_LIMIT),
+            collective_id=0, has_side_effects=True, vmem_limit_bytes=VMEM_LIMIT - held),
     )(resid_buf, shuffle.reshape(1, T), mlp_out, enc_weight[0], dec_weight[0], enc_bias, dec_bias)
-    fc = 512 if F % 512 == 0 else KC
     enc_grad, dec_grad, bgrad, rebuilt = pl.pallas_call(
         functools.partial(weight_kernel, float(T) ** (-0.5)),
-        grid=(F // fc,),
         out_shape=(
             shape((F, H), BF), shape((F, 2, H), BF), shape((1, F), f32), shape((R, 2, 2 * H), BF)),
-        in_specs=[
-            pl.BlockSpec((T, fc), lambda i: (0, i)), pl.BlockSpec((T, fc), lambda i: (0, i)),
-            pl.BlockSpec((2, T, H), lambda i: (0, 0, 0)), pl.BlockSpec((T, H), lambda i: (0, 0)),
-            pl.BlockSpec((2 * R, 2 * H), lambda i: (0, 0))],
-        out_specs=(
-            pl.BlockSpec((fc, H), lambda i: (i, 0)), pl.BlockSpec((fc, 2, H), lambda i: (i, 0, 0)),
-            pl.BlockSpec((1, fc), lambda i: (0, i)), pl.BlockSpec((R, 2, 2 * H), lambda i: (0, 0, 0))),
-        compiler_params=pltpu.CompilerParams(vmem_limit_bytes=VMEM_LIMIT),
-    )(feats, gpre, errs, xs, parts)
+        in_specs=[vm] * 5,
+        out_specs=(hbm, hbm, vm, vm),
+        scratch_shapes=[
+            pltpu.VMEM((2, 2 * KC, H), BF), pltpu.VMEM((2, KC, H), BF), dma((2,)), dma((2,))],
+        compiler_params=pltpu.CompilerParams(vmem_limit_bytes=VMEM_LIMIT // 2),
+    )(fx, gpre, errs, xs, parts)
     return rebuilt, enc_grad[None], dec_grad[None], bgrad
 
 

time: 141 us -> 135 us (0.957)
  Pallas kernels: 140 us -> 134 us
    pallas_call x2, Pallas kernels: 140 us -> 134 us  [the longest x1 116 us: fused(): pl.pallas_call(functools.partial(step_kernel, n, J), out_shape=tuple((plt...]
where the time goes in v1:
time: 135 us
  Pallas kernels  134 us (99%)
    pallas_call x1, Pallas kernels, fused(): pl.pallas_call(functools.partial(step_kernel, n, J), out_shape=tuple((plt...  116 us
    pallas_call x1, Pallas kernels, fused(): pl.pallas_call(functools.partial(weight_kernel, float(T) ** (-0.5)), out_...  17.6 us

profile of v1, /device:TPU:0, one launch (start us, length us, event | category | flops | bytes accessed | tf_op | source)
XLA Modules:
  0.0 134.8 jit_solution(15457589644247790921)
XLA Ops:
  0.6 116.4 %shard_map.102 = (bf16[4096,512]{1,0:T(8,128)(2,1)S(1)}, bf16[256,2304]{1,0:T(8,128)(2,1)S(1)}, bf16[2,256,2304]{2,1,0:T(8,128)(2,1)S(1)}, bf16[256,2048]{1,0:T(8,128)(2,1)S(1)}, bf16[64,4608]{1,0:T(8,128)(2,1)S(1)}) custom-call(bf16[32,2,4608]{2,1,0:T(2,128)(2,1)} %res.1, s32[1,256]{1,0:T(1,128)} %bitcast.7, bf16[32,2,4608]{2,1,0:T(2,128)(2,1)} %mlp.1, ...), custom_call_target="tpu_custom_call" | custom-call | tf_op jit(solution)/shard_map/pallas_call | solution.py:560
  117.1 17.6 %shard_map.103 = (bf16[2048,2304]{1,0:T(8,128)(2,1)}, bf16[2048,2,2304]{2,1,0:T(2,128)(2,1)}, f32[1,2048]{1,0:T(1,128)}, bf16[32,2,4608]{2,1,0:T(2,128)(2,1)}) custom-call(bf16[4096,512]{1,0:T(8,128)(2,1)S(1)} %get-tuple-element.13.fx, bf16[256,2048]{1,0:T(8,128)(2,1)S(1)} %get-tuple-element.14.gpre, bf16[2,256,2304]{2,1,0:T(8,128)(2,1)S(1)} %get-tuple-element.15.errs, ...), custom_call_target="tpu_custom_call" | custom-call | tf_op jit(solution)/shard_map/pallas_call | solution.py:585

commit v2 on v1

v2 whole, which is shorter than its diff:
```python
import functools
import math

import jax
import jax.numpy as jnp
from jax import lax
from jax.experimental import pallas as pl
from jax.experimental.pallas import tpu as pltpu
from jax.sharding import PartitionSpec as P

LAYERS = 2


def from_behind(block, axis, distance):
    devices = range(lax.axis_size(axis))
    route = [(i - distance, i) for i in devices if i - distance in devices]
    return lax.ppermute(block, axis, route)


def dot_last(left, right):
    return lax.dot_general(
        left, right, (((1,), (1,)), ((), ())), preferred_element_type=jnp.float32
    )


def dot_first(left, right):
    return lax.dot_general(
        left, right, (((0,), (0,)), ((), ())), preferred_element_type=jnp.float32
    )


def on_device(resid_buf, shuffle, mlp_out, enc_weight, dec_weight, enc_bias, dec_bias):
    feat_count = lax.axis_size("feat")
    row_count = lax.axis_size("row")
    sub_blocks = lax.axis_size("layer") // LAYERS
    layer_pos = lax.axis_index("layer")
    row_pos = lax.axis_index("row")
    source = layer_pos // sub_blocks
    rows_each = resid_buf.shape[0]
    width = dec_bias.shape[1]
    half_width = enc_weight.shape[2]
    local_rows = rows_each * feat_count
    total_rows = local_rows * row_count
    loss_scale = float(total_rows) ** (-0.5)
    own_layer = lax.dynamic_index_in_dim(resid_buf, source, axis=1, keepdims=False)
    buffer_all = lax.all_gather(own_layer, ("feat", "row"), axis=0, tiled=True)
    batch_rows = jnp.take(buffer_all, shuffle, axis=0)
    blocks = batch_rows.reshape(feat_count, row_count, rows_each, width)
    inputs_half = lax.dynamic_slice_in_dim(
        jnp.swapaxes(blocks, 0, 1), row_pos * half_width, half_width, axis=3
    )
    inputs_half = inputs_half.reshape(total_rows, half_width)
    own_half_dec = dec_weight[0][:, 0]
    next_half_dec = dec_weight[0][:, 1]
    pre_all = lax.psum(dot_last(inputs_half, enc_weight[0]), "row") + enc_bias[0]
    features_all = jnp.maximum(pre_all, 0.0).astype(jnp.bfloat16)
    own_part = jnp.dot(features_all, own_half_dec, preferred_element_type=jnp.float32)
    next_part = jnp.dot(features_all, next_half_dec, preferred_element_type=jnp.float32)
    carried = from_behind(next_part, "layer", sub_blocks)
    spread = (own_part + carried).reshape(row_count, local_rows, half_width)
    halves = lax.psum_scatter(spread, "feat", scatter_dimension=1, tiled=True)
    joined = lax.all_to_all(halves, "row", split_axis=0, concat_axis=2, tiled=True)
    section_sum = joined.reshape(rows_each, width)
    target_ids = jnp.arange(LAYERS, dtype=jnp.int32)
    target_slots = jnp.where((target_ids == source)[:, None, None], section_sum[None], 0.0)
    totals = lax.psum(target_slots, "layer")
    recon_sum = jnp.swapaxes(totals, 0, 1) + dec_bias[None]
    errors = (recon_sum - mlp_out.astype(jnp.float32)).astype(jnp.bfloat16)
    gathered = lax.all_gather(errors, ("feat", "row"), axis=0, tiled=True)
    error_grid = gathered.reshape(feat_count, row_count, rows_each, LAYERS, width)
    errors_mine = lax.dynamic_index_in_dim(error_grid, row_pos, axis=1, keepdims=False)
    errors_mine = errors_mine.reshape(local_rows, LAYERS, width)
    errors_half = lax.dynamic_slice_in_dim(
        jnp.swapaxes(error_grid, 0, 1), row_pos * half_width, half_width, axis=4
    )
    errors_half = errors_half.reshape(total_rows, LAYERS, half_width)
    live_next = source + 1 < LAYERS
    next_index = jnp.minimum(source + 1, LAYERS - 1)
    half_own = lax.dynamic_index_in_dim(errors_half, source, axis=1, keepdims=False)
    half_next = lax.dynamic_index_in_dim(errors_half, next_index, axis=1, keepdims=False)
    half_next = jnp.where(live_next, half_next, jnp.zeros_like(half_next))
    half_terms = dot_last(half_own, own_half_dec) + dot_last(half_next, next_half_dec)
    grad_feats = lax.psum(half_terms, "row") * loss_scale
    grad_all = jnp.where(pre_all > 0, grad_feats, 0.0).astype(jnp.bfloat16)
    grad_own = loss_scale * dot_first(features_all, half_own)
    grad_next = loss_scale * dot_first(features_all, half_next)
    enc_grad = dot_first(grad_all, inputs_half).astype(jnp.bfloat16)
    dec_grad = jnp.stack([grad_own, grad_next], axis=1).astype(jnp.bfloat16)
    bias_grad = jnp.sum(grad_all.astype(jnp.float32), axis=0)
    return (recon_sum.astype(jnp.bfloat16), enc_grad[None], dec_grad[None], bias_grad[None])

KC = 256
DC = 128
MESH = pl.DeviceIdType.MESH
VMEM_LIMIT = 67043328
BF = jnp.bfloat16


def pick(rows, cols, stride, offset):
    r = lax.broadcasted_iota(jnp.int32, (rows, cols), 0)
    c = lax.broadcasted_iota(jnp.int32, (rows, cols), 1)
    return (c == stride * r + offset).astype(BF)


def spread_to(offset):
    r = lax.broadcasted_iota(jnp.int32, (2 * DC, DC), 0)
    c = lax.broadcasted_iota(jnp.int32, (2 * DC, DC), 1)
    return (r == 2 * c + offset).astype(BF)


def mm(left, right):
    return jnp.dot(left, right, preferred_element_type=jnp.float32)


def halves_of(width):
    return next(q for q in (3, 2, 1) if width % (q * DC) == 0)


def step_kernel(
    n, J, res, shuf, mlp, enc, dec, bias, dbias,
    fx, xs, e, gpre, parts,
    enc_v, wv, raw, xsend, xg, mlpx, msend, dsel, pre, pre_recv, feats,
    nsend, nrecv, facc, osend, rr, rl, rc, rb, gacc, g_recv,
    sem_l, sem_raw, x_s, x_r, y_s, m_s, m_r, p_s, p_r, f_s, f_r, n_s, n_r,
    rs_s, rs_r, a_s, a_r, t_s, t_r, b_s, b_r, g_s, g_r, q_s, q_r,
):
    z = lax.axis_index("feat")
    x = lax.axis_index("layer")
    c = lax.axis_index("row")
    Q, R, HX = xsend.shape[1:]
    F, H = enc_v.shape
    T = xs.shape[0]
    T2, CR, NC = T // 2, 2 * R, H // J
    nk, slots = F // KC, raw.shape[0]
    scale = float(T) ** (-0.5)
    other_c, other_x = 1 - c, 1 - x

    def far(dz):
        return lax.rem(z + dz, n)

    def back(dz):
        return lax.rem(z + n - dz, n)

    def remote(src, dst, send, recv, **where):
        return pltpu.make_async_remote_copy(
            src_ref=src, dst_ref=dst, send_sem=send, recv_sem=recv,
            device_id=where, device_id_type=MESH)

    def unless_ends(dz, act):
        if dz == n - 1:
            pl.when(z != 0)(act)
        elif dz == 1:
            pl.when(z != n - 1)(act)
        else:
            act()

    def relays(act):
        pl.when(z == 2)(lambda: act(1, 3))
        pl.when(z == 1)(lambda: act(3, 1))

    def raw_copy(i, slot):
        return pltpu.make_async_copy(
            dec.reshape(2 * F, H).at[pl.ds(pl.multiple_of(i * 2 * DC, 2 * DC), 2 * DC)], raw.at[slot], sem_raw.at[slot])

    nd = F // DC
    for i in range(slots - 1):
        raw_copy(i, i).start()
    enc_copy = pltpu.make_async_copy(enc, enc_v, sem_l)
    enc_copy.start()

    barrier = pltpu.get_barrier_semaphore()
    for dz in range(n):
        if dz:
            pl.semaphore_signal(barrier, inc=1, device_id={"feat": far(dz), "row": c}, device_id_type=MESH)
        pl.semaphore_signal(barrier, inc=1, device_id={"feat": far(dz), "row": other_c}, device_id_type=MESH)
    for cc in (c, other_c):
        pl.semaphore_signal(barrier, inc=1, device_id={"layer": other_x, "row": cc}, device_id_type=MESH)

    own_x = mm(pick(R, 2 * R, 2, x), res.reshape(2 * R, 2 * H)[...]).astype(BF)
    x_mine = jnp.where(c == 0, own_x[:, :H], own_x[:, H:])
    x_other = jnp.where(c == 0, own_x[:, H:], own_x[:, :H])
    for q in range(Q):
        xsend[0, q] = x_mine[:, q * HX:(q + 1) * HX]
        xsend[1, q] = x_other[:, q * HX:(q + 1) * HX]
        xg[z, c, q] = x_mine[:, q * HX:(q + 1) * HX]
    own_m = mm(pick(R, 2 * R, 2, x), mlp.reshape(2 * R, 2 * H)[...]).astype(BF)
    mlpx[c] = jnp.where(c == 0, own_m[:, :H], own_m[:, H:])
    msend[...] = jnp.where(c == 0, own_m[:, H:], own_m[:, :H])

    pl.semaphore_wait(barrier, 2 * n + 1)

    def x_copy(dz, k, q):
        return remote(xsend.at[k, q], xg.at[z, c, q], x_s.at[dz, k, q], x_r.at[dz, k, q],
                      feat=far(dz), row=c if k == 0 else other_c)

    x_list = [(dz, k) for dz in (2, 1, 3) for k in range(2)] + [(0, 1)]
    for q in range(Q):
        for dz, k in x_list:
            unless_ends(dz, lambda: x_copy(dz, k, q).start())

    def y_copy(k, q, to, at):
        cc = c if k == 0 else other_c
        return remote(xg.at[back(2), cc, q], xg.at[back(2), cc, q], y_s.at[k, q], x_r.at[at, k, q], feat=far(to))

    m_copy = remote(msend, mlpx.at[c], m_s, m_r, row=other_c)
    m_copy.start()
    d_all = jnp.where(x == 0, dbias[0:1, :], dbias[1:2, :])
    dsel[...] = jnp.where(c == 0, d_all[:, :H], d_all[:, H:])

    apart = jnp.concatenate([pick(DC, 2 * DC, 2, 0), pick(DC, 2 * DC, 2, 1)], axis=0)

    def split_body(i, carry):
        slot = lax.rem(i, slots)

        @pl.when(i + slots - 1 < nd)
        def _():
            raw_copy(i + slots - 1, lax.rem(i + slots - 1, slots)).start()

        raw_copy(i, slot).wait()
        both = mm(apart, raw[slot]).astype(BF)
        rows = pl.ds(pl.multiple_of(i * DC, DC), DC)
        wv[0, rows, :] = both[:DC]
        wv[1, rows, :] = both[DC:]
        return carry

    def pass_on(q):
        for k in range(2):
            x_copy(2, k, q).wait_recv()
            relays(lambda to, at: y_copy(k, q, to, at).start())

    perm = (lax.broadcasted_iota(jnp.int32, (T, T), 0) == shuf[...]).astype(BF)

    def p_copy(k):
        return remote(pre.at[k, pl.ds(pl.multiple_of(other_c * T2, T2), T2)], pre_recv.at[k], p_s.at[k], p_r.at[k], row=other_c)

    mine = pl.ds(pl.multiple_of(c * T2, T2), T2)

    def f_copy(k):
        return remote(feats.at[k, mine], feats.at[k, mine], f_s.at[k], f_r.at[k], row=other_c)

    lax.fori_loop(0, nd // 2, split_body, 0)
    pass_on(0)
    lax.fori_loop(nd // 2, nd, split_body, 0)
    enc_copy.wait()
    per = 2 if nk % 2 == 0 else 1
    for q in range(Q):
        if q:
            pass_on(q)
        for dz, k in x_list:
            if dz != 2:
                x_copy(dz, k, q).wait_recv()
        lo = q * HX
        xs[:, lo:lo + HX] = dot_first(perm, xg[:, :, q].reshape(T, HX)).astype(BF)

        def pre_body(i, carry):
            rows = pl.ds(pl.multiple_of(i * per * KC, KC), per * KC)
            v = dot_last(xs[:, lo:lo + HX], enc_v[rows, lo:lo + HX])
            for h in range(per):
                part = v[:, h * KC:(h + 1) * KC]
                k = i * per + h
                pre[k] = part if q == 0 else pre[k] + part
                if q == Q - 1:
                    p_copy(k).start()
            return carry

        lax.fori_loop(0, nk // per, pre_body, 0)

    def feat_body(k, carry):
        p_copy(k).wait_recv()
        cols = pl.ds(pl.multiple_of(k * KC, KC), KC)
        v = pre[k, mine, :] + pre_recv[k] + bias[:, cols]
        feats[k, mine, :] = jnp.maximum(v, 0.0).astype(BF)
        f_copy(k).start()
        return carry

    lax.fori_loop(0, nk, feat_body, 0)

    def zero_body(k, carry):
        gacc[k] = jnp.zeros((T, KC), jnp.float32)
        f_copy(k).wait_recv()
        return carry

    lax.fori_loop(0, nk, zero_body, 0)
    m_copy.wait_recv()
    up0, up1 = spread_to(0), spread_to(1)

    def expand(b):
        rows = pl.ds(pl.multiple_of(b * 2 * DC, 2 * DC), 2 * DC)
        turned = feats[b // (KC // DC), :, pl.ds(pl.multiple_of(lax.rem(b, KC // DC) * DC, DC), DC)].T
        fx[rows, :T] = mm(up0, turned).astype(BF)
        fx[rows, T:] = mm(up1, turned).astype(BF)

    def n_copy(j):
        return remote(nsend.at[j], nrecv.at[j], n_s.at[j], n_r.at[j], layer=other_x)

    def right_copy(j, k):
        some = pl.ds(k + 1, n - 1 - k)
        return remote(osend.at[j, some], rr.at[j, some], rs_s.at[j, 0], rs_r.at[j, 0], feat=k + 1)

    def left_copy(j, k):
        some = pl.ds(0, k)
        return remote(osend.at[j, some], rl.at[j, some], rs_s.at[j, 1], rs_r.at[j, 1], feat=k - 1)

    def wide(j):
        return pl.ds(pl.multiple_of(j * NC, NC), NC)

    def all_feats():
        return jnp.concatenate([feats[k] for k in range(nk)], axis=1)

    def front(j):
        @pl.when(x == 0)
        def _():
            nsend[j] = mm(all_feats(), wv[1, :, wide(j)]).astype(BF)
            n_copy(j).start()

        facc[j] = mm(all_feats(), wv[0, :, wide(j)]).reshape(n, CR, NC)

        @pl.when(x == 1)
        def _():
            n_copy(j).wait_recv()
            facc[j] = facc[j] + nrecv[j].astype(jnp.float32).reshape(n, CR, NC)

        @pl.when(z == 0)
        def _():
            osend[j, 1:] = facc[j, 1:].astype(BF)
            right_copy(j, 0).start()

        @pl.when(z == n - 1)
        def _():
            osend[j, :n - 1] = facc[j, :n - 1].astype(BF)
            left_copy(j, n - 1).start()

    def go_right(j, k):
        right_copy(j, k - 1).wait_recv()
        osend[j, k + 1:] = (facc[j, k + 1:] + rr[j, k + 1:].astype(jnp.float32)).astype(BF)
        right_copy(j, k).start()

    def go_left(j, k):
        left_copy(j, k + 1).wait_recv()
        osend[j, :k] = (facc[j, :k] + rl[j, :k].astype(jnp.float32)).astype(BF)
        left_copy(j, k).start()

    def relay_near(j):
        pl.when(z == 1)(lambda: go_right(j, 1))
        pl.when(z == 2)(lambda: go_left(j, 2))

    def relay_far(j):
        pl.when(z == 2)(lambda: go_right(j, 2))
        pl.when(z == 1)(lambda: go_left(j, 1))

    def a_copy(j, b, way):
        to = jnp.minimum(z + 1, n - 1) if way == 0 else jnp.maximum(z - 1, 0)
        return remote(e.at[j, 0, b], e.at[j, 0, b], a_s.at[j, way, b], a_r.at[j, b], feat=to)

    def t_copy(j, b):
        return remote(e.at[j, 0, b], e.at[j, 1, b], t_s.at[j, b], t_r.at[j, b], layer=other_x)

    def final(j):
        @pl.when(z == 0)
        def _():
            left_copy(j, 1).wait_recv()

        @pl.when(z == n - 1)
        def _():
            right_copy(j, n - 2).wait_recv()

        @pl.when(z > 0)
        def _():
            facc[j, z] = facc[j, z] + rr[j, z].astype(jnp.float32)

        @pl.when(z < n - 1)
        def _():
            facc[j, z] = facc[j, z] + rl[j, z].astype(jnp.float32)

        total = facc[j, z] + dsel[:, wide(j)]
        e[j, 0, z] = (total - mlpx[:, :, wide(j)].reshape(CR, NC).astype(jnp.float32)).astype(BF)
        pl.when(z < n - 1)(lambda: a_copy(j, z, 0).start())
        pl.when(z > 0)(lambda: a_copy(j, z, 1).start())
        pl.when(x == 1)(lambda: t_copy(j, z).start())
        kept = total.astype(BF).reshape(2, R, NC)
        rc[0, j] = kept[0]
        rc[1, j] = kept[1]

    def hop(j, h):
        @pl.when(z >= h)
        def _():
            a_copy(j, z - h, 0).wait_recv()
            pl.when(z < n - 1)(lambda: a_copy(j, z - h, 0).start())
            pl.when(x == 1)(lambda: t_copy(j, z - h).start())

        @pl.when(z + h < n)
        def _():
            a_copy(j, z + h, 1).wait_recv()
            pl.when(z > 0)(lambda: a_copy(j, z + h, 1).start())
            pl.when(x == 1)(lambda: t_copy(j, z + h).start())

    def g_copy(k):
        return remote(gacc.at[k, pl.ds(pl.multiple_of(other_c * T2, T2), T2)], g_recv.at[k], g_s.at[k], g_r.at[k], row=other_c)

    def grads(j):
        last = j == J - 1

        @pl.when(x == 0)
        def _():
            for b in range(n):
                t_copy(j, b).wait_recv()

            def body(k, carry):
                rows = pl.ds(pl.multiple_of(k * KC, KC), KC)
                gacc[k] = (gacc[k] + dot_last(e[j, 0].reshape(T, NC), wv[0, rows, wide(j)])
                           + dot_last(e[j, 1].reshape(T, NC), wv[1, rows, wide(j)]))
                pl.when(last)(lambda: g_copy(k).start())
                return carry

            lax.fori_loop(0, nk, body, 0)

        @pl.when(x == 1)
        def _():
            def body(k, carry):
                rows = pl.ds(pl.multiple_of(k * KC, KC), KC)
                gacc[k] = gacc[k] + dot_last(e[j, 0].reshape(T, NC), wv[0, rows, wide(j)])
                pl.when(last)(lambda: g_copy(k).start())
                return carry

            lax.fori_loop(0, nk, body, 0)

    def early_b(j):
        pl.when(j == JB - 1)(lambda: [b_copy(k, 0).start() for k in range(1, 4)] and None)

    JB = min(3, J - 1)

    def b_copy(k, late):
        dx, dc = k // 2, k % 2
        to_x = other_x if dx else x
        to_c = other_c if dc else c
        some = pl.ds(JB, J - JB) if late else pl.ds(0, JB)
        return remote(rc.at[to_c, some], rb.at[x, c, some], b_s.at[k, late], b_r.at[k, late], layer=to_x, row=to_c)

    stages = ((0, front), (1, relay_near), (2, relay_far), (3, final), (3, early_b),
              (4, lambda j: hop(j, 1)), (5, lambda j: hop(j, 2)), (6, lambda j: hop(j, 3)), (7, grads))
    steps = J + stages[-1][0]
    share = pl.cdiv(nd, steps)

    def pipe(s, carry):
        for lag, act in stages:
            pl.when(jnp.logical_and(s >= lag, s < J + lag))(functools.partial(act, s - lag))
        for i in range(share):
            pl.when(s * share + i < nd)(functools.partial(expand, s * share + i))
        return carry

    lax.fori_loop(0, steps, pipe, 0)
    for k in range(1, 4):
        b_copy(k, 1).start()

    def q_copy(k):
        return remote(gpre.at[k, mine], gpre.at[k, mine], q_s.at[k], q_r.at[k], row=other_c)

    def mask_body(k, carry):
        g_copy(k).wait_recv()
        v = (gacc[k, mine, :] + g_recv[k]) * scale
        gpre[k, mine, :] = jnp.where(feats[k, mine, :].astype(jnp.float32) > 0, v, 0.0).astype(BF)
        q_copy(k).start()
        return carry

    lax.fori_loop(0, nk, mask_body, 0)
    rb[x, c] = rc[c]

    def sent_body(k, carry):
        p_copy(k).wait_send()
        f_copy(k).wait_send()
        return carry

    lax.fori_loop(0, nk, sent_body, 0)
    for q in range(Q):
        for dz, k in x_list:
            unless_ends(dz, lambda: x_copy(dz, k, q).wait_send())
        for k in range(2):
            relays(lambda to, at: y_copy(k, q, to, at).wait_send())
    m_copy.wait_send()

    def sent_chunk(j, carry):
        for k in range(n):
            @pl.when(z == k)
            def _():
                if k < n - 1:
                    right_copy(j, k).wait_send()
                if k > 0:
                    left_copy(j, k).wait_send()

        for b in range(n):
            pl.when(jnp.logical_and(z >= b, z < n - 1))(lambda: a_copy(j, b, 0).wait_send())
            pl.when(jnp.logical_and(z <= b, z > 0))(lambda: a_copy(j, b, 1).wait_send())

        @pl.when(x == 0)
        def _():
            n_copy(j).wait_send()

        @pl.when(x == 1)
        def _():
            for b in range(n):
                t_copy(j, b).wait_send()

        return carry

    lax.fori_loop(0, J, sent_chunk, 0)
    for k in range(1, 4):
        for late in range(2):
            b_copy(k, late).wait_recv()
    for h in range(2):
        for j in range(J):
            lo = h * H + j * NC
            parts[:, lo:lo + NC] = rb[:, h, j].reshape(2 * R, NC)

    def last_body(k, carry):
        q_copy(k).wait_recv()
        g_copy(k).wait_send()
        q_copy(k).wait_send()
        return carry

    lax.fori_loop(0, nk, last_body, 0)
    for k in range(1, 4):
        for late in range(2):
            b_copy(k, late).wait_send()


def weight_kernel(scale, fx, gpre, e, xs, parts, enc_grad, dec_grad, bgrad, rebuilt, dbuf, ebuf, dsem, esem):
    nb, T, _ = gpre.shape
    H = xs.shape[1]
    J, NC = e.shape[0], e.shape[-1]
    R2 = parts.shape[0]
    x = lax.axis_index("layer")

    def d_copy(i, slot):
        rows = pl.ds(pl.multiple_of(i * 2 * KC, 2 * KC), 2 * KC)
        return pltpu.make_async_copy(dbuf.at[slot], dec_grad.reshape(2 * nb * KC, H).at[rows], dsem.at[slot])

    def e_copy(i, slot):
        rows = pl.ds(pl.multiple_of(i * KC, KC), KC)
        return pltpu.make_async_copy(ebuf.at[slot], enc_grad.at[rows], esem.at[slot])

    def block(i, carry):
        slot = lax.rem(i, 2)

        @pl.when(i >= 2)
        def _():
            d_copy(i - 2, slot).wait()
            e_copy(i - 2, slot).wait()

        rows = pl.ds(pl.multiple_of(i * 2 * KC, 2 * KC), 2 * KC)

        @pl.when(x == 0)
        def _():
            for j in range(J):
                dbuf[slot, :, j * NC:(j + 1) * NC] = (scale * mm(fx[rows, :], e[j].reshape(2 * T, NC))).astype(BF)

        @pl.when(x == 1)
        def _():
            for j in range(J):
                dbuf[slot, :, j * NC:(j + 1) * NC] = (scale * mm(fx[rows, :T], e[j, 0].reshape(T, NC))).astype(BF)

        d_copy(i, slot).start()
        ebuf[slot] = dot_first(gpre[i], xs[...]).astype(BF)
        e_copy(i, slot).start()
        bgrad[:, pl.ds(pl.multiple_of(i * KC, KC), KC)] = jnp.sum(gpre[i].astype(jnp.float32), axis=0, keepdims=True)
        return carry

    lax.fori_loop(0, nb, block, 0)
    i = lax.broadcasted_iota(jnp.int32, (R2, R2), 0)
    j = lax.broadcasted_iota(jnp.int32, (R2, R2), 1)
    inter = (j == (i % 2) * (R2 // 2) + i // 2).astype(BF)
    rebuilt.reshape(R2, 2 * H)[...] = mm(inter, parts[...]).astype(BF)
    for k in range(max(nb - 2, 0), nb):
        d_copy(k, k % 2).wait()
        e_copy(k, k % 2).wait()


def fused(resid_buf, shuffle, mlp_out, enc_weight, dec_weight, enc_bias, dec_bias):
    n = lax.axis_size("feat")
    R = resid_buf.shape[0]
    F, H = enc_weight.shape[1:]
    T = R * n * 2
    T2, CR = T // 2, 2 * R
    J = H // KC
    NC, nk = H // J, F // KC
    Q = halves_of(H)
    HX = H // Q
    f32 = jnp.float32
    vm = pl.BlockSpec(memory_space=pltpu.VMEM)
    hbm = pl.BlockSpec(memory_space=pl.ANY)
    dma = pltpu.SemaphoreType.DMA
    vmem = pltpu.VMEM
    shape = jax.ShapeDtypeStruct
    outs = ((2 * F, 2 * T), (T, H), (J, 2, n, CR, NC), (nk, T, KC), (2 * R, 2 * H))
    held = sum(2 * math.prod(a) for a in outs)
    fx, xs, e, gpre, parts = pl.pallas_call(
        functools.partial(step_kernel, n, J),
        out_shape=tuple(vmem(a, BF) for a in outs),
        in_specs=[vm, vm, vm, hbm, hbm, vm, vm],
        out_specs=(vm,) * 5,
        scratch_shapes=[
            vmem((F, H), BF), vmem((2, F, H), BF), vmem((4, 2 * DC, H), BF),
            vmem((2, Q, R, HX), BF), vmem((n, 2, Q, R, HX), BF),
            vmem((2, R, H), BF), vmem((R, H), BF), vmem((1, H), f32),
            vmem((nk, T, KC), f32), vmem((nk, T2, KC), f32), vmem((nk, T, KC), BF),
            vmem((J, T, NC), BF), vmem((J, T, NC), BF), vmem((J, n, CR, NC), f32),
            vmem((J, n, CR, NC), BF), vmem((J, n, CR, NC), BF), vmem((J, n, CR, NC), BF),
            vmem((2, J, R, NC), BF), vmem((2, 2, J, R, NC), BF),
            vmem((nk, T, KC), f32), vmem((nk, T2, KC), f32),
            dma, dma((4,)), dma((n, 2, Q)), dma((n, 2, Q)), dma((2, Q)), dma, dma,
            dma((nk,)), dma((nk,)), dma((nk,)), dma((nk,)), dma((J,)), dma((J,)),
            dma((J, 2)), dma((J, 2)), dma((J, 2, n)), dma((J, n)), dma((J, n)), dma((J, n)),
            dma((4, 2)), dma((4, 2)), dma((nk,)), dma((nk,)), dma((nk,)), dma((nk,)),
        ],
        compiler_params=pltpu.CompilerParams(
            collective_id=0, has_side_effects=True, vmem_limit_bytes=VMEM_LIMIT - held),
    )(resid_buf, shuffle.reshape(1, T), mlp_out, enc_weight[0], dec_weight[0], enc_bias, dec_bias)
    enc_grad, dec_grad, bgrad, rebuilt = pl.pallas_call(
        functools.partial(weight_kernel, float(T) ** (-0.5)),
        out_shape=(
            shape((F, H), BF), shape((F, 2, H), BF), shape((1, F), f32), shape((R, 2, 2 * H), BF)),
        in_specs=[vm] * 5,
        out_specs=(hbm, hbm, vm, vm),
        scratch_shapes=[
            vmem((2, 2 * KC, H), BF), vmem((2, KC, H), BF), dma((2,)), dma((2,))],
        compiler_params=pltpu.CompilerParams(vmem_limit_bytes=VMEM_LIMIT // 2),
    )(fx, gpre, e, xs, parts)
    return rebuilt, enc_grad[None], dec_grad[None], bgrad


def chosen(resid_buf, shuffle, mlp_out, enc_weight, dec_weight, enc_bias, dec_bias):
    args = (resid_buf, shuffle, mlp_out, enc_weight, dec_weight, enc_bias, dec_bias)
    rows, width = resid_buf.shape[0], enc_weight.shape[2]
    fits = (
        lax.axis_size("layer") == LAYERS == 2 and lax.axis_size("row") == 2
        and lax.axis_size("feat") == 4 and rows % 16 == 0
        and width % KC == 0 and enc_weight.shape[1] % KC == 0)
    return fused(*args) if fits else on_device(*args)


def solution(mesh):
    return jax.shard_map(
        chosen,
        mesh=mesh,
        in_specs=(
            P(("groups", "feat", "row"), None, None),
            P("groups"),
            P(("groups", "feat", "row"), None, None),
            P("layer", "feat", "row"),
            P("layer", "feat", None, "row"),
            P("layer", "feat"),
            P(),
        ),
        out_specs=(
            P(("groups", "feat", "row"), None, None),
            P(("groups", "layer"), "feat", "row"),
            P(("groups", "layer"), "feat", None, "row"),
            P(("groups", "layer"), "feat"),
        ),
        check_vma=False,
    )
```

time: 135 us -> 120 us (0.89)
  Pallas kernels: 134 us -> 120 us
    pallas_call x1, Pallas kernels: 116 us -> 102 us  [fused(): pl.pallas_call(functools.partial(step_kernel, n, J), out_shape=tuple((vme...]
where the time goes in v2:
time: 120 us
  Pallas kernels  120 us (100%)
    pallas_call x1, Pallas kernels, fused(): pl.pallas_call(functools.partial(step_kernel, n, J), out_shape=tuple((vme...  102 us
    pallas_call x1, Pallas kernels, fused(): pl.pallas_call(functools.partial(weight_kernel, float(T) ** (-0.5)), out_...  17.5 us

profile of v2, /device:TPU:0, one launch (start us, length us, event | category | flops | bytes accessed | tf_op | source)
XLA Modules:
  0.0 120.3 jit_solution(11736880669817827758)
XLA Ops:
  0.6 102.1 %shard_map.102 = (bf16[4096,512]{1,0:T(8,128)(2,1)S(1)}, bf16[256,2304]{1,0:T(8,128)(2,1)S(1)}, bf16[9,2,4,64,256]{4,3,2,1,0:T(8,128)(2,1)S(1)}, bf16[8,256,256]{2,1,0:T(8,128)(2,1)S(1)}, bf16[64,4608]{1,0:T(8,128)(2,1)S(1)}) custom-call(bf16[32,2,4608]{2,1,0:T(2,128)(2,1)} %res.1, s32[1,256]{1,0:T(1,128)} %bitcast.7, bf16[32,2,4608]{2,1,0:T(2,128)(2,1)} %mlp.1, ...), custom_call_target="tpu_custom_call" | custom-call | tf_op jit(solution)/shard_map/pallas_call | solution.py:595
  102.7 17.5 %shard_map.103 = (bf16[2048,2304]{1,0:T(8,128)(2,1)}, bf16[2048,2,2304]{2,1,0:T(2,128)(2,1)}, f32[1,2048]{1,0:T(1,128)}, bf16[32,2,4608]{2,1,0:T(2,128)(2,1)}) custom-call(bf16[4096,512]{1,0:T(8,128)(2,1)S(1)} %get-tuple-element.13.fx, bf16[8,256,256]{2,1,0:T(8,128)(2,1)S(1)} %get-tuple-element.14.gpre, bf16[9,2,4,64,256]{4,3,2,1,0:T(8,128)(2,1)S(1)} %get-tuple-element.15.e, ...), custom_call_target="tpu_custom_call" | custom-call | tf_op jit(solution)/shard_map/pallas_call | solution.py:617

commit v3 on v2

--- a/solution.py
+++ b/solution.py
@@ -91,6 +91,8 @@
 
 KC = 256
 DC = 128
+GC = 1024
+LAG0 = 9
 MESH = pl.DeviceIdType.MESH
 VMEM_LIMIT = 67043328
 BF = jnp.bfloat16
@@ -118,8 +120,8 @@
 
 def step_kernel(
     n, J, res, shuf, mlp, enc, dec, bias, dbias,
-    fx, xs, e, gpre, parts,
-    enc_v, wv, raw, xsend, xg, mlpx, msend, dsel, pre, pre_recv, feats,
+    dg, xs, gt, parts,
+    fx, e, enc_v, raw, xsend, xg, mlpx, msend, dsel, pre, pre_recv, feats,
     nsend, nrecv, facc, osend, rr, rl, rc, rb, gacc, g_recv,
     sem_l, sem_raw, x_s, x_r, y_s, m_s, m_r, p_s, p_r, f_s, f_r, n_s, n_r,
     rs_s, rs_r, a_s, a_r, t_s, t_r, b_s, b_r, g_s, g_r, q_s, q_r,
@@ -219,8 +221,8 @@
         raw_copy(i, slot).wait()
         both = mm(apart, raw[slot]).astype(BF)
         rows = pl.ds(pl.multiple_of(i * DC, DC), DC)
-        wv[0, rows, :] = both[:DC]
-        wv[1, rows, :] = both[DC:]
+        dg[rows, :] = both[:DC]
+        dg[pl.ds(pl.multiple_of(F + i * DC, DC), DC), :] = both[DC:]
         return carry
 
     def pass_on(q):
@@ -275,8 +277,11 @@
 
     lax.fori_loop(0, nk, feat_body, 0)
 
+    def rows_of(k, size, base=0):
+        return pl.ds(pl.multiple_of(base + k * size, KC), size)
+
     def zero_body(k, carry):
-        gacc[k] = jnp.zeros((T, KC), jnp.float32)
+        gacc[:, rows_of(k, KC), :] = jnp.zeros((2, KC, T2), jnp.float32)
         f_copy(k).wait_recv()
         return carry
 
@@ -307,13 +312,16 @@
     def all_feats():
         return jnp.concatenate([feats[k] for k in range(nk)], axis=1)
 
+    def send_next(j):
+        @pl.when(x == 0)
+        def _():
+            nsend[j] = mm(all_feats(), dg[pl.ds(F, F), wide(j)]).astype(BF)
+            n_copy(j).start()
+
     def front(j):
-        @pl.when(x == 0)
-        def _():
-            nsend[j] = mm(all_feats(), wv[1, :, wide(j)]).astype(BF)
-            n_copy(j).start()
-
-        facc[j] = mm(all_feats(), wv[0, :, wide(j)]).reshape(n, CR, NC)
+        for i in range(2):
+            pl.when(2 * j + i < J)(functools.partial(send_next, 2 * j + i))
+        facc[j] = mm(all_feats(), dg[pl.ds(0, F), wide(j)]).reshape(n, CR, NC)
 
         @pl.when(x == 1)
         def _():
@@ -395,74 +403,104 @@
             pl.when(x == 1)(lambda: t_copy(j, z + h).start())
 
     def g_copy(k):
-        return remote(gacc.at[k, pl.ds(pl.multiple_of(other_c * T2, T2), T2)], g_recv.at[k], g_s.at[k], g_r.at[k], row=other_c)
+        return remote(gacc.at[other_c, rows_of(k, GC)], g_recv.at[rows_of(k, GC)], g_s.at[k], g_r.at[k], row=other_c)
 
     def grads(j):
         last = j == J - 1
 
-        @pl.when(x == 0)
-        def _():
-            for b in range(n):
-                t_copy(j, b).wait_recv()
-
-            def body(k, carry):
-                rows = pl.ds(pl.multiple_of(k * KC, KC), KC)
-                gacc[k] = (gacc[k] + dot_last(e[j, 0].reshape(T, NC), wv[0, rows, wide(j)])
-                           + dot_last(e[j, 1].reshape(T, NC), wv[1, rows, wide(j)]))
-                pl.when(last)(lambda: g_copy(k).start())
-                return carry
-
-            lax.fori_loop(0, nk, body, 0)
-
-        @pl.when(x == 1)
-        def _():
-            def body(k, carry):
-                rows = pl.ds(pl.multiple_of(k * KC, KC), KC)
-                gacc[k] = gacc[k] + dot_last(e[j, 0].reshape(T, NC), wv[0, rows, wide(j)])
-                pl.when(last)(lambda: g_copy(k).start())
-                return carry
-
-            lax.fori_loop(0, nk, body, 0)
-
-    def early_b(j):
-        pl.when(j == JB - 1)(lambda: [b_copy(k, 0).start() for k in range(1, 4)] and None)
-
-    JB = min(3, J - 1)
-
-    def b_copy(k, late):
+        def body(k, carry):
+            rows = rows_of(k, GC)
+            v = dot_last(dg[rows, wide(j)], e[j, 0].reshape(T, NC))
+            gacc[0, rows, :] = gacc[0, rows, :] + v[:, :T2]
+            gacc[1, rows, :] = gacc[1, rows, :] + v[:, T2:]
+            pl.when(last)(lambda: g_copy(k).start())
+            return carry
+
+        lax.fori_loop(0, F // GC, body, 0)
+
+    def both_grads(j):
+        last = j == J - 1
+        for b in range(n):
+            t_copy(j, b).wait_recv()
+
+        def body(k, carry):
+            rows, below = rows_of(k, GC), rows_of(k, GC, F)
+            v = dot_last(dg[rows, wide(j)], e[j, 0].reshape(T, NC)) + dot_last(dg[below, wide(j)], e[j, 1].reshape(T, NC))
+            gacc[0, rows, :] = gacc[0, rows, :] + v[:, :T2]
+            gacc[1, rows, :] = gacc[1, rows, :] + v[:, T2:]
+            pl.when(last)(lambda: g_copy(k).start())
+            return carry
+
+        lax.fori_loop(0, F // GC, body, 0)
+
+    def weights(j):
+        def body(k, carry):
+            rows = rows_of(k, 2 * GC)
+            dg[rows, wide(j)] = (scale * mm(fx[rows, :T], e[j, 0].reshape(T, NC))).astype(BF)
+            return carry
+
+        lax.fori_loop(0, F // GC, body, 0)
+
+    def both_weights(j):
+        def body(k, carry):
+            rows = rows_of(k, 2 * GC)
+            dg[rows, wide(j)] = (scale * mm(fx[rows, :], e[j].reshape(2 * T, NC))).astype(BF)
+            return carry
+
+        lax.fori_loop(0, F // GC, body, 0)
+
+    cuts = (0, J // 3, 2 * J // 3, J)
+
+    def b_copy(k, p):
         dx, dc = k // 2, k % 2
         to_x = other_x if dx else x
         to_c = other_c if dc else c
-        some = pl.ds(JB, J - JB) if late else pl.ds(0, JB)
-        return remote(rc.at[to_c, some], rb.at[x, c, some], b_s.at[k, late], b_r.at[k, late], layer=to_x, row=to_c)
-
-    stages = ((0, front), (1, relay_near), (2, relay_far), (3, final), (3, early_b),
-              (4, lambda j: hop(j, 1)), (5, lambda j: hop(j, 2)), (6, lambda j: hop(j, 3)), (7, grads))
-    steps = J + stages[-1][0]
-    share = pl.cdiv(nd, steps)
+        some = pl.ds(cuts[p], cuts[p + 1] - cuts[p])
+        return remote(rc.at[to_c, some], rb.at[x, c, some], b_s.at[k, p], b_r.at[k, p], layer=to_x, row=to_c)
+
+    def start_b(p):
+        for k in range(1, 4):
+            b_copy(k, p).start()
+
+    def early_b(j):
+        for p in range(2):
+            pl.when(j == cuts[p + 1] - 1)(functools.partial(start_b, p))
+
+    def late_b(j):
+        pl.when(j == J - 1)(lambda: start_b(2))
+
+    stages = (
+        (0, None, front), (1, None, relay_near), (2, None, relay_far), (3, None, final), (3, None, early_b),
+        (4, None, lambda j: hop(j, 1)), (5, None, lambda j: hop(j, 2)), (6, None, lambda j: hop(j, 3)), (6, None, late_b),
+        (7, 1, grads), (LAG0, 0, both_grads), (8, 1, weights), (LAG0 + 1, 0, both_weights))
+    steps = J + LAG0 + 1
+    share = pl.cdiv(nd, 8)
 
     def pipe(s, carry):
-        for lag, act in stages:
-            pl.when(jnp.logical_and(s >= lag, s < J + lag))(functools.partial(act, s - lag))
+        for lag, side, act in stages:
+            live = jnp.logical_and(s >= lag, s < J + lag)
+            if side is not None:
+                live = jnp.logical_and(live, x == side)
+            pl.when(live)(functools.partial(act, s - lag))
         for i in range(share):
             pl.when(s * share + i < nd)(functools.partial(expand, s * share + i))
         return carry
 
     lax.fori_loop(0, steps, pipe, 0)
-    for k in range(1, 4):
-        b_copy(k, 1).start()
 
     def q_copy(k):
-        return remote(gpre.at[k, mine], gpre.at[k, mine], q_s.at[k], q_r.at[k], row=other_c)
+        return remote(gt.at[c, rows_of(k, GC)], gt.at[c, rows_of(k, GC)], q_s.at[k], q_r.at[k], row=other_c)
 
     def mask_body(k, carry):
         g_copy(k).wait_recv()
-        v = (gacc[k, mine, :] + g_recv[k]) * scale
-        gpre[k, mine, :] = jnp.where(feats[k, mine, :].astype(jnp.float32) > 0, v, 0.0).astype(BF)
+        rows = rows_of(k, GC)
+        seen = jnp.concatenate([feats[k * (GC // KC) + i, mine, :] for i in range(GC // KC)], axis=1).T
+        v = (gacc[c, rows, :] + g_recv[rows, :]) * scale
+        gt[c, rows, :] = jnp.where(seen.astype(jnp.float32) > 0, v, 0.0).astype(BF)
         q_copy(k).start()
         return carry
 
-    lax.fori_loop(0, nk, mask_body, 0)
+    lax.fori_loop(0, F // GC, mask_body, 0)
     rb[x, c] = rc[c]
 
     def sent_body(k, carry):
@@ -504,12 +542,15 @@
 
     lax.fori_loop(0, J, sent_chunk, 0)
     for k in range(1, 4):
-        for late in range(2):
-            b_copy(k, late).wait_recv()
+        for p in range(3):
+            b_copy(k, p).wait_recv()
     for h in range(2):
         for j in range(J):
             lo = h * H + j * NC
             parts[:, lo:lo + NC] = rb[:, h, j].reshape(2 * R, NC)
+    for k in range(1, 4):
+        for p in range(3):
+            b_copy(k, p).wait_send()
 
     def last_body(k, carry):
         q_copy(k).wait_recv()
@@ -517,61 +558,52 @@
         q_copy(k).wait_send()
         return carry
 
-    lax.fori_loop(0, nk, last_body, 0)
-    for k in range(1, 4):
-        for late in range(2):
-            b_copy(k, late).wait_send()
-
-
-def weight_kernel(scale, fx, gpre, e, xs, parts, enc_grad, dec_grad, bgrad, rebuilt, dbuf, ebuf, dsem, esem):
-    nb, T, _ = gpre.shape
+    lax.fori_loop(0, F // GC, last_body, 0)
+
+
+def weight_kernel(dg, gt, xs, parts, enc_grad, dec_grad, bgrad, rebuilt, ebuf, bbuf, rbuf, dsem, esem, bsem, rsem):
+    F, T2 = gt.shape[1:]
     H = xs.shape[1]
-    J, NC = e.shape[0], e.shape[-1]
     R2 = parts.shape[0]
-    x = lax.axis_index("layer")
-
-    def d_copy(i, slot):
-        rows = pl.ds(pl.multiple_of(i * 2 * KC, 2 * KC), 2 * KC)
-        return pltpu.make_async_copy(dbuf.at[slot], dec_grad.reshape(2 * nb * KC, H).at[rows], dsem.at[slot])
-
-    def e_copy(i, slot):
-        rows = pl.ds(pl.multiple_of(i * KC, KC), KC)
-        return pltpu.make_async_copy(ebuf.at[slot], enc_grad.at[rows], esem.at[slot])
-
-    def block(i, carry):
-        slot = lax.rem(i, 2)
-
-        @pl.when(i >= 2)
-        def _():
-            d_copy(i - 2, slot).wait()
-            e_copy(i - 2, slot).wait()
-
-        rows = pl.ds(pl.multiple_of(i * 2 * KC, 2 * KC), 2 * KC)
-
-        @pl.when(x == 0)
-        def _():
-            for j in range(J):
-                dbuf[slot, :, j * NC:(j + 1) * NC] = (scale * mm(fx[rows, :], e[j].reshape(2 * T, NC))).astype(BF)
-
-        @pl.when(x == 1)
-        def _():
-            for j in range(J):
-                dbuf[slot, :, j * NC:(j + 1) * NC] = (scale * mm(fx[rows, :T], e[j, 0].reshape(T, NC))).astype(BF)
-
-        d_copy(i, slot).start()
-        ebuf[slot] = dot_first(gpre[i], xs[...]).astype(BF)
-        e_copy(i, slot).start()
-        bgrad[:, pl.ds(pl.multiple_of(i * KC, KC), KC)] = jnp.sum(gpre[i].astype(jnp.float32), axis=0, keepdims=True)
-        return carry
-
-    lax.fori_loop(0, nb, block, 0)
+    nb = F // KC
+
+    def rows_of(i, size):
+        return pl.ds(pl.multiple_of(i * size, size), size)
+
+    def d_copy(i):
+        rows = rows_of(i, 2 * KC)
+        return pltpu.make_async_copy(dg.at[rows], dec_grad.reshape(2 * F, H).at[rows], dsem.at[i])
+
+    def e_copy(i):
+        rows = rows_of(i, KC)
+        return pltpu.make_async_copy(ebuf.at[rows], enc_grad.at[rows], esem.at[i])
+
+    b_copy = pltpu.make_async_copy(bbuf, bgrad, bsem)
+    r_copy = pltpu.make_async_copy(rbuf, rebuilt.reshape(R2, 2 * H), rsem)
+    for i in range(nb):
+        d_copy(i).start()
     i = lax.broadcasted_iota(jnp.int32, (R2, R2), 0)
     j = lax.broadcasted_iota(jnp.int32, (R2, R2), 1)
     inter = (j == (i % 2) * (R2 // 2) + i // 2).astype(BF)
-    rebuilt.reshape(R2, 2 * H)[...] = mm(inter, parts[...]).astype(BF)
-    for k in range(max(nb - 2, 0), nb):
-        d_copy(k, k % 2).wait()
-        e_copy(k, k % 2).wait()
+    rbuf[...] = mm(inter, parts[...]).astype(BF)
+    r_copy.start()
+    ones = jnp.ones((8, 2 * T2), BF)
+
+    def block(i, carry):
+        rows = rows_of(i, KC)
+        g = jnp.concatenate([gt[0, rows, :], gt[1, rows, :]], axis=1)
+        ebuf[rows, :] = mm(g, xs[...]).astype(BF)
+        e_copy(i).start()
+        bbuf[:, rows] = dot_last(ones, g)[0:1]
+        return carry
+
+    lax.fori_loop(0, nb, block, 0)
+    b_copy.start()
+    for i in range(nb):
+        d_copy(i).wait()
+        e_copy(i).wait()
+    r_copy.wait()
+    b_copy.wait()
 
 
 def fused(resid_buf, shuffle, mlp_out, enc_weight, dec_weight, enc_bias, dec_bias):
@@ -590,40 +622,40 @@
     dma = pltpu.SemaphoreType.DMA
     vmem = pltpu.VMEM
     shape = jax.ShapeDtypeStruct
-    outs = ((2 * F, 2 * T), (T, H), (J, 2, n, CR, NC), (nk, T, KC), (2 * R, 2 * H))
+    outs = ((2 * F, H), (T, H), (2, F, T2), (2 * R, 2 * H))
     held = sum(2 * math.prod(a) for a in outs)
-    fx, xs, e, gpre, parts = pl.pallas_call(
+    dg, xs, gt, parts = pl.pallas_call(
         functools.partial(step_kernel, n, J),
         out_shape=tuple(vmem(a, BF) for a in outs),
         in_specs=[vm, vm, vm, hbm, hbm, vm, vm],
-        out_specs=(vm,) * 5,
+        out_specs=(vm,) * 4,
         scratch_shapes=[
-            vmem((F, H), BF), vmem((2, F, H), BF), vmem((4, 2 * DC, H), BF),
+            vmem((2 * F, 2 * T), BF), vmem((J, 2, n, CR, NC), BF), vmem((F, H), BF), vmem((4, 2 * DC, H), BF),
             vmem((2, Q, R, HX), BF), vmem((n, 2, Q, R, HX), BF),
             vmem((2, R, H), BF), vmem((R, H), BF), vmem((1, H), f32),
             vmem((nk, T, KC), f32), vmem((nk, T2, KC), f32), vmem((nk, T, KC), BF),
             vmem((J, T, NC), BF), vmem((J, T, NC), BF), vmem((J, n, CR, NC), f32),
             vmem((J, n, CR, NC), BF), vmem((J, n, CR, NC), BF), vmem((J, n, CR, NC), BF),
             vmem((2, J, R, NC), BF), vmem((2, 2, J, R, NC), BF),
-            vmem((nk, T, KC), f32), vmem((nk, T2, KC), f32),
+            vmem((2, F, T2), f32), vmem((F, T2), f32),
             dma, dma((4,)), dma((n, 2, Q)), dma((n, 2, Q)), dma((2, Q)), dma, dma,
             dma((nk,)), dma((nk,)), dma((nk,)), dma((nk,)), dma((J,)), dma((J,)),
             dma((J, 2)), dma((J, 2)), dma((J, 2, n)), dma((J, n)), dma((J, n)), dma((J, n)),
-            dma((4, 2)), dma((4, 2)), dma((nk,)), dma((nk,)), dma((nk,)), dma((nk,)),
+            dma((4, 3)), dma((4, 3)), dma((nk,)), dma((nk,)), dma((nk,)), dma((nk,)),
         ],
         compiler_params=pltpu.CompilerParams(
             collective_id=0, has_side_effects=True, vmem_limit_bytes=VMEM_LIMIT - held),
     )(resid_buf, shuffle.reshape(1, T), mlp_out, enc_weight[0], dec_weight[0], enc_bias, dec_bias)
     enc_grad, dec_grad, bgrad, rebuilt = pl.pallas_call(
-        functools.partial(weight_kernel, float(T) ** (-0.5)),
+        weight_kernel,
         out_shape=(
             shape((F, H), BF), shape((F, 2, H), BF), shape((1, F), f32), shape((R, 2, 2 * H), BF)),
-        in_specs=[vm] * 5,
-        out_specs=(hbm, hbm, vm, vm),
+        in_specs=[vm] * 4,
+        out_specs=(hbm,) * 4,
         scratch_shapes=[
-            vmem((2, 2 * KC, H), BF), vmem((2, KC, H), BF), dma((2,)), dma((2,))],
-        compiler_params=pltpu.CompilerParams(vmem_limit_bytes=VMEM_LIMIT // 2),
-    )(fx, gpre, e, xs, parts)
+            vmem((F, H), BF), vmem((1, F), f32), vmem((2 * R, 2 * H), BF), dma((nk,)), dma((nk,)), dma, dma],
+        compiler_params=pltpu.CompilerParams(vmem_limit_bytes=VMEM_LIMIT // 3),
+    )(dg, gt, xs, parts)
     return rebuilt, enc_grad[None], dec_grad[None], bgrad
 
 
@@ -633,7 +665,7 @@
     fits = (
         lax.axis_size("layer") == LAYERS == 2 and lax.axis_size("row") == 2
         and lax.axis_size("feat") == 4 and rows % 16 == 0
-        and width % KC == 0 and enc_weight.shape[1] % KC == 0)
+        and width % KC == 0 and width // KC >= 3 and enc_weight.shape[1] % GC == 0)
     return fused(*args) if fits else on_device(*args)
 
 

time: 120 us -> 107 us (0.89)
  Pallas kernels: 120 us -> 106 us
    pallas_call x1, Pallas kernels: 17.5 us -> 9.65 us  [fused(): pl.pallas_call(weight_kernel, out_shape=(shape((F, H), BF), shape((F, 2,...]
    pallas_call x1, Pallas kernels: 102 us -> 96.7 us  [fused(): pl.pallas_call(functools.partial(step_kernel, n, J), out_shape=tuple((vme...]
where the time goes in v3:
time: 107 us
  Pallas kernels  106 us (99%)
    pallas_call x1, Pallas kernels, fused(): pl.pallas_call(functools.partial(step_kernel, n, J), out_shape=tuple((vme...  96.7 us
    pallas_call x1, Pallas kernels, fused(): pl.pallas_call(weight_kernel, out_shape=(shape((F, H), BF), shape((F, 2,...  9.65 us

profile of v3, /device:TPU:0, one launch (start us, length us, event | category | flops | bytes accessed | tf_op | source)
XLA Modules:
  0.0 107.0 jit_solution(11753818495267515261)
XLA Ops:
  0.6 96.7 %shard_map.102 = (bf16[4096,2304]{1,0:T(8,128)(2,1)S(1)}, bf16[256,2304]{1,0:T(8,128)(2,1)S(1)}, bf16[2,2048,128]{2,1,0:T(8,128)(2,1)S(1)}, bf16[64,4608]{1,0:T(8,128)(2,1)S(1)}) custom-call(bf16[32,2,4608]{2,1,0:T(2,128)(2,1)} %res.1, s32[1,256]{1,0:T(1,128)} %bitcast.7, bf16[32,2,4608]{2,1,0:T(2,128)(2,1)} %mlp.1, bf16[2048,2304]{1,0:T(8,128)(2,1)} %bitcast.6, ...), custom_call_target="tpu_custom_call" | custom-call | tf_op jit(solution)/shard_map/pallas_call | solution.py:627
  97.4 9.7 %shard_map.103 = (bf16[2048,2304]{1,0:T(8,128)(2,1)}, bf16[2048,2,2304]{2,1,0:T(2,128)(2,1)}, f32[1,2048]{1,0:T(1,128)}, bf16[32,2,4608]{2,1,0:T(2,128)(2,1)}) custom-call(bf16[4096,2304]{1,0:T(8,128)(2,1)S(1)} %get-tuple-element.12.dg, bf16[2,2048,128]{2,1,0:T(8,128)(2,1)S(1)} %get-tuple-element.13.gt, bf16[256,2304]{1,0:T(8,128)(2,1)S(1)} %get-tuple-element.14.xs, ...), custom_call_target="tpu_custom_call" | custom-call | tf_op jit(solution)/shard_map/pallas_call | solution.py:649

commit v4 on v3

--- a/solution.py
+++ b/solution.py
@@ -92,7 +92,8 @@
 KC = 256
 DC = 128
 GC = 1024
-LAG0 = 9
+LAG0 = 8
+LAG1 = 7
 MESH = pl.DeviceIdType.MESH
 VMEM_LIMIT = 67043328
 BF = jnp.bfloat16
@@ -192,7 +193,7 @@
     pl.semaphore_wait(barrier, 2 * n + 1)
 
     def x_copy(dz, k, q):
-        return remote(xsend.at[k, q], xg.at[z, c, q], x_s.at[dz, k, q], x_r.at[dz, k, q],
+        return remote(xsend.at[k, q], xg.at[z, c, q], x_s.at[dz, k], x_r.at[dz, k, q],
                       feat=far(dz), row=c if k == 0 else other_c)
 
     x_list = [(dz, k) for dz in (2, 1, 3) for k in range(2)] + [(0, 1)]
@@ -202,7 +203,7 @@
 
     def y_copy(k, q, to, at):
         cc = c if k == 0 else other_c
-        return remote(xg.at[back(2), cc, q], xg.at[back(2), cc, q], y_s.at[k, q], x_r.at[at, k, q], feat=far(to))
+        return remote(xg.at[back(2), cc, q], xg.at[back(2), cc, q], y_s.at[k], x_r.at[at, k, q], feat=far(to))
 
     m_copy = remote(msend, mlpx.at[c], m_s, m_r, row=other_c)
     m_copy.start()
@@ -233,12 +234,12 @@
     perm = (lax.broadcasted_iota(jnp.int32, (T, T), 0) == shuf[...]).astype(BF)
 
     def p_copy(k):
-        return remote(pre.at[k, pl.ds(pl.multiple_of(other_c * T2, T2), T2)], pre_recv.at[k], p_s.at[k], p_r.at[k], row=other_c)
+        return remote(pre.at[k, pl.ds(pl.multiple_of(other_c * T2, T2), T2)], pre_recv.at[k], p_s, p_r.at[k], row=other_c)
 
     mine = pl.ds(pl.multiple_of(c * T2, T2), T2)
 
     def f_copy(k):
-        return remote(feats.at[k, mine], feats.at[k, mine], f_s.at[k], f_r.at[k], row=other_c)
+        return remote(feats.at[k, mine], feats.at[k, mine], f_s, f_r, row=other_c)
 
     lax.fori_loop(0, nd // 2, split_body, 0)
     pass_on(0)
@@ -282,10 +283,11 @@
 
     def zero_body(k, carry):
         gacc[:, rows_of(k, KC), :] = jnp.zeros((2, KC, T2), jnp.float32)
-        f_copy(k).wait_recv()
         return carry
 
     lax.fori_loop(0, nk, zero_body, 0)
+    all_f = remote(feats.at[:, mine], feats.at[:, mine], f_s, f_r, row=other_c)
+    all_f.wait_recv()
     m_copy.wait_recv()
     up0, up1 = spread_to(0), spread_to(1)
 
@@ -293,18 +295,39 @@
         rows = pl.ds(pl.multiple_of(b * 2 * DC, 2 * DC), 2 * DC)
         turned = feats[b // (KC // DC), :, pl.ds(pl.multiple_of(lax.rem(b, KC // DC) * DC, DC), DC)].T
         fx[rows, :T] = mm(up0, turned).astype(BF)
-        fx[rows, T:] = mm(up1, turned).astype(BF)
+
+        @pl.when(x == 0)
+        def _():
+            fx[rows, T:] = mm(up1, turned).astype(BF)
 
     def n_copy(j):
-        return remote(nsend.at[j], nrecv.at[j], n_s.at[j], n_r.at[j], layer=other_x)
-
-    def right_copy(j, k):
-        some = pl.ds(k + 1, n - 1 - k)
-        return remote(osend.at[j, some], rr.at[j, some], rs_s.at[j, 0], rs_r.at[j, 0], feat=k + 1)
-
-    def left_copy(j, k):
-        some = pl.ds(0, k)
-        return remote(osend.at[j, some], rl.at[j, some], rs_s.at[j, 1], rs_r.at[j, 1], feat=k - 1)
+        return remote(nsend.at[j], nrecv.at[j], n_s, n_r.at[j], layer=other_x)
+
+    def right_copy(j, k, onward):
+        some = pl.ds(k + 2, n - 2 - k) if onward else pl.ds(k + 1, 1)
+        return remote(osend.at[j, some], rr.at[j, some], rs_s.at[0], rs_r.at[j, 0, onward], feat=k + 1)
+
+    def left_copy(j, k, onward):
+        some = pl.ds(0, k - 1) if onward else pl.ds(k - 1, 1)
+        return remote(osend.at[j, some], rl.at[j, some], rs_s.at[1], rs_r.at[j, 1, onward], feat=k - 1)
+
+    def send_right(j, k):
+        for lo, hi, onward in ((k + 2, n, 1), (k + 1, k + 2, 0)):
+            if lo < hi:
+                v = facc[j, lo:hi]
+                if k > 0:
+                    v = v + rr[j, lo:hi].astype(jnp.float32)
+                osend[j, lo:hi] = v.astype(BF)
+                right_copy(j, k, onward).start()
+
+    def send_left(j, k):
+        for lo, hi, onward in ((0, k - 1, 1), (k - 1, k, 0)):
+            if lo < hi:
+                v = facc[j, lo:hi]
+                if k < n - 1:
+                    v = v + rl[j, lo:hi].astype(jnp.float32)
+                osend[j, lo:hi] = v.astype(BF)
+                left_copy(j, k, onward).start()
 
     def wide(j):
         return pl.ds(pl.multiple_of(j * NC, NC), NC)
@@ -328,25 +351,16 @@
             n_copy(j).wait_recv()
             facc[j] = facc[j] + nrecv[j].astype(jnp.float32).reshape(n, CR, NC)
 
-        @pl.when(z == 0)
-        def _():
-            osend[j, 1:] = facc[j, 1:].astype(BF)
-            right_copy(j, 0).start()
-
-        @pl.when(z == n - 1)
-        def _():
-            osend[j, :n - 1] = facc[j, :n - 1].astype(BF)
-            left_copy(j, n - 1).start()
+        pl.when(z == 0)(lambda: send_right(j, 0))
+        pl.when(z == n - 1)(lambda: send_left(j, n - 1))
 
     def go_right(j, k):
-        right_copy(j, k - 1).wait_recv()
-        osend[j, k + 1:] = (facc[j, k + 1:] + rr[j, k + 1:].astype(jnp.float32)).astype(BF)
-        right_copy(j, k).start()
+        right_copy(j, k - 1, 1).wait_recv()
+        send_right(j, k)
 
     def go_left(j, k):
-        left_copy(j, k + 1).wait_recv()
-        osend[j, :k] = (facc[j, :k] + rl[j, :k].astype(jnp.float32)).astype(BF)
-        left_copy(j, k).start()
+        left_copy(j, k + 1, 1).wait_recv()
+        send_left(j, k)
 
     def relay_near(j):
         pl.when(z == 1)(lambda: go_right(j, 1))
@@ -358,19 +372,19 @@
 
     def a_copy(j, b, way):
         to = jnp.minimum(z + 1, n - 1) if way == 0 else jnp.maximum(z - 1, 0)
-        return remote(e.at[j, 0, b], e.at[j, 0, b], a_s.at[j, way, b], a_r.at[j, b], feat=to)
+        return remote(e.at[j, 0, b], e.at[j, 0, b], a_s.at[way], a_r.at[j, b], feat=to)
 
     def t_copy(j, b):
-        return remote(e.at[j, 0, b], e.at[j, 1, b], t_s.at[j, b], t_r.at[j, b], layer=other_x)
+        return remote(e.at[j, 0, b], e.at[j, 1, b], t_s, t_r.at[j], layer=other_x)
 
     def final(j):
-        @pl.when(z == 0)
-        def _():
-            left_copy(j, 1).wait_recv()
-
-        @pl.when(z == n - 1)
-        def _():
-            right_copy(j, n - 2).wait_recv()
+        for k in range(n):
+            @pl.when(z == k)
+            def _():
+                if k > 0:
+                    right_copy(j, k - 1, 0).wait_recv()
+                if k < n - 1:
+                    left_copy(j, k + 1, 0).wait_recv()
 
         @pl.when(z > 0)
         def _():
@@ -403,7 +417,7 @@
             pl.when(x == 1)(lambda: t_copy(j, z + h).start())
 
     def g_copy(k):
-        return remote(gacc.at[other_c, rows_of(k, GC)], g_recv.at[rows_of(k, GC)], g_s.at[k], g_r.at[k], row=other_c)
+        return remote(gacc.at[other_c, rows_of(k, GC)], g_recv.at[rows_of(k, GC)], g_s, g_r.at[k], row=other_c)
 
     def grads(j):
         last = j == J - 1
@@ -420,8 +434,7 @@
 
     def both_grads(j):
         last = j == J - 1
-        for b in range(n):
-            t_copy(j, b).wait_recv()
+        remote(e.at[j, 0], e.at[j, 1], t_s, t_r.at[j], layer=other_x).wait_recv()
 
         def body(k, carry):
             rows, below = rows_of(k, GC), rows_of(k, GC, F)
@@ -455,8 +468,8 @@
         dx, dc = k // 2, k % 2
         to_x = other_x if dx else x
         to_c = other_c if dc else c
-        some = pl.ds(cuts[p], cuts[p + 1] - cuts[p])
-        return remote(rc.at[to_c, some], rb.at[x, c, some], b_s.at[k, p], b_r.at[k, p], layer=to_x, row=to_c)
+        some = pl.ds(0, J) if p is None else pl.ds(cuts[p], cuts[p + 1] - cuts[p])
+        return remote(rc.at[to_c, some], rb.at[x, c, some], b_s.at[k], b_r.at[k], layer=to_x, row=to_c)
 
     def start_b(p):
         for k in range(1, 4):
@@ -472,9 +485,9 @@
     stages = (
         (0, None, front), (1, None, relay_near), (2, None, relay_far), (3, None, final), (3, None, early_b),
         (4, None, lambda j: hop(j, 1)), (5, None, lambda j: hop(j, 2)), (6, None, lambda j: hop(j, 3)), (6, None, late_b),
-        (7, 1, grads), (LAG0, 0, both_grads), (8, 1, weights), (LAG0 + 1, 0, both_weights))
-    steps = J + LAG0 + 1
-    share = pl.cdiv(nd, 8)
+        (LAG1, 1, grads), (LAG1 + 1, 1, weights), (LAG0, 0, both_grads), (LAG0, 0, both_weights))
+    steps = J + max(LAG0, LAG1 + 1)
+    share = pl.cdiv(nd, LAG0)
 
     def pipe(s, carry):
         for lag, side, act in stages:
@@ -483,13 +496,21 @@
                 live = jnp.logical_and(live, x == side)
             pl.when(live)(functools.partial(act, s - lag))
         for i in range(share):
-            pl.when(s * share + i < nd)(functools.partial(expand, s * share + i))
+            pl.when(jnp.logical_and(x == 0, s * share + i < nd))(functools.partial(expand, s * share + i))
         return carry
 
+    @pl.when(x == 1)
+    def _():
+        def body(b, carry):
+            expand(b)
+            return carry
+
+        lax.fori_loop(0, nd, body, 0)
+
     lax.fori_loop(0, steps, pipe, 0)
 
     def q_copy(k):
-        return remote(gt.at[c, rows_of(k, GC)], gt.at[c, rows_of(k, GC)], q_s.at[k], q_r.at[k], row=other_c)
+        return remote(gt.at[c, rows_of(k, GC)], gt.at[c, rows_of(k, GC)], q_s, q_r.at[k], row=other_c)
 
     def mask_body(k, carry):
         g_copy(k).wait_recv()
@@ -503,62 +524,55 @@
     lax.fori_loop(0, F // GC, mask_body, 0)
     rb[x, c] = rc[c]
 
-    def sent_body(k, carry):
-        p_copy(k).wait_send()
-        f_copy(k).wait_send()
-        return carry
-
-    lax.fori_loop(0, nk, sent_body, 0)
-    for q in range(Q):
-        for dz, k in x_list:
-            unless_ends(dz, lambda: x_copy(dz, k, q).wait_send())
-        for k in range(2):
-            relays(lambda to, at: y_copy(k, q, to, at).wait_send())
+    theirs = pl.ds(pl.multiple_of(other_c * T2, T2), T2)
+    remote(pre.at[:, theirs], pre_recv, p_s, p_r.at[0], row=other_c).wait_send()
+    all_f.wait_send()
     m_copy.wait_send()
 
-    def sent_chunk(j, carry):
-        for k in range(n):
-            @pl.when(z == k)
-            def _():
-                if k < n - 1:
-                    right_copy(j, k).wait_send()
-                if k > 0:
-                    left_copy(j, k).wait_send()
-
-        for b in range(n):
-            pl.when(jnp.logical_and(z >= b, z < n - 1))(lambda: a_copy(j, b, 0).wait_send())
-            pl.when(jnp.logical_and(z <= b, z > 0))(lambda: a_copy(j, b, 1).wait_send())
-
-        @pl.when(x == 0)
-        def _():
-            n_copy(j).wait_send()
-
-        @pl.when(x == 1)
-        def _():
-            for b in range(n):
-                t_copy(j, b).wait_send()
-
-        return carry
-
-    lax.fori_loop(0, J, sent_chunk, 0)
+    def x_all(dz, k):
+        return remote(xsend.at[k], xg.at[z, c], x_s.at[dz, k], x_r.at[dz, k, 0], feat=far(dz), row=other_c)
+
+    for dz, k in x_list:
+        unless_ends(dz, lambda: x_all(dz, k).wait_send())
+
+    def y_all(k, to, at):
+        cc = c if k == 0 else other_c
+        return remote(xg.at[back(2), cc], xg.at[back(2), cc], y_s.at[k], x_r.at[at, k, 0], feat=far(to))
+
+    for k in range(2):
+        relays(lambda to, at: y_all(k, to, at).wait_send())
+
+    def sent(src, sem, **where):
+        remote(src, src, sem, a_r.at[0, 0], **where).wait_send()
+
+    for k in range(n):
+        @pl.when(z == k)
+        def _():
+            if k < n - 1:
+                sent(osend.at[:, pl.ds(k + 1, n - 1 - k)], rs_s.at[0], feat=k + 1)
+                sent(e.at[:, 0, pl.ds(0, k + 1)], a_s.at[0], feat=k + 1)
+            if k > 0:
+                sent(osend.at[:, pl.ds(0, k)], rs_s.at[1], feat=k - 1)
+                sent(e.at[:, 0, pl.ds(k, n - k)], a_s.at[1], feat=k - 1)
+
+    pl.when(x == 0)(lambda: sent(nsend, n_s, layer=other_x))
+    pl.when(x == 1)(lambda: sent(e.at[:, 0], t_s, layer=other_x))
     for k in range(1, 4):
-        for p in range(3):
-            b_copy(k, p).wait_recv()
+        b_copy(k, None).wait_recv()
     for h in range(2):
         for j in range(J):
             lo = h * H + j * NC
             parts[:, lo:lo + NC] = rb[:, h, j].reshape(2 * R, NC)
     for k in range(1, 4):
-        for p in range(3):
-            b_copy(k, p).wait_send()
+        b_copy(k, None).wait_send()
 
     def last_body(k, carry):
         q_copy(k).wait_recv()
-        g_copy(k).wait_send()
-        q_copy(k).wait_send()
         return carry
 
     lax.fori_loop(0, F // GC, last_body, 0)
+    sent(gacc.at[other_c], g_s, row=other_c)
+    sent(gt.at[c], q_s, row=other_c)
 
 
 def weight_kernel(dg, gt, xs, parts, enc_grad, dec_grad, bgrad, rebuilt, ebuf, bbuf, rbuf, dsem, esem, bsem, rsem):
@@ -638,10 +652,10 @@
             vmem((J, n, CR, NC), BF), vmem((J, n, CR, NC), BF), vmem((J, n, CR, NC), BF),
             vmem((2, J, R, NC), BF), vmem((2, 2, J, R, NC), BF),
             vmem((2, F, T2), f32), vmem((F, T2), f32),
-            dma, dma((4,)), dma((n, 2, Q)), dma((n, 2, Q)), dma((2, Q)), dma, dma,
-            dma((nk,)), dma((nk,)), dma((nk,)), dma((nk,)), dma((J,)), dma((J,)),
-            dma((J, 2)), dma((J, 2)), dma((J, 2, n)), dma((J, n)), dma((J, n)), dma((J, n)),
-            dma((4, 3)), dma((4, 3)), dma((nk,)), dma((nk,)), dma((nk,)), dma((nk,)),
+            dma, dma((4,)), dma((n, 2)), dma((n, 2, Q)), dma((2,)), dma, dma,
+            dma, dma((nk,)), dma, dma, dma, dma((J,)),
+            dma((2,)), dma((J, 2, 2)), dma((2,)), dma((J, n)), dma, dma((J,)),
+            dma((4,)), dma((4,)), dma, dma((F // GC,)), dma, dma((F // GC,)),
         ],
         compiler_params=pltpu.CompilerParams(
             collective_id=0, has_side_effects=True, vmem_limit_bytes=VMEM_LIMIT - held),

time: 107 us -> 103 us (0.963)
  Pallas kernels: 106 us -> 102 us
    pallas_call x1, Pallas kernels: 96.7 us -> 92.3 us  [fused(): pl.pallas_call(functools.partial(step_kernel, n, J), out_shape=tuple((vme...]
where the time goes in v4:
time: 103 us
  Pallas kernels  102 us (99%)
    pallas_call x1, Pallas kernels, fused(): pl.pallas_call(functools.partial(step_kernel, n, J), out_shape=tuple((vme...  92.3 us
    pallas_call x1, Pallas kernels, fused(): pl.pallas_call(weight_kernel, out_shape=(shape((F, H), BF), shape((F, 2,...  9.65 us

profile of v4, /device:TPU:0, one launch (start us, length us, event | category | flops | bytes accessed | tf_op | source)
XLA Modules:
  0.0 102.6 jit_solution(2888943301252502192)
XLA Ops:
  0.6 92.3 %shard_map.102 = (bf16[4096,2304]{1,0:T(8,128)(2,1)S(1)}, bf16[256,2304]{1,0:T(8,128)(2,1)S(1)}, bf16[2,2048,128]{2,1,0:T(8,128)(2,1)S(1)}, bf16[64,4608]{1,0:T(8,128)(2,1)S(1)}) custom-call(bf16[32,2,4608]{2,1,0:T(2,128)(2,1)} %res.1, s32[1,256]{1,0:T(1,128)} %bitcast.7, bf16[32,2,4608]{2,1,0:T(2,128)(2,1)} %mlp.1, bf16[2048,2304]{1,0:T(8,128)(2,1)} %bitcast.6, ...), custom_call_target="tpu_custom_call" | custom-call | tf_op jit(solution)/shard_map/pallas_call | solution.py:641
  93.0 9.7 %shard_map.103 = (bf16[2048,2304]{1,0:T(8,128)(2,1)}, bf16[2048,2,2304]{2,1,0:T(2,128)(2,1)}, f32[1,2048]{1,0:T(1,128)}, bf16[32,2,4608]{2,1,0:T(2,128)(2,1)}) custom-call(bf16[4096,2304]{1,0:T(8,128)(2,1)S(1)} %get-tuple-element.12.dg, bf16[2,2048,128]{2,1,0:T(8,128)(2,1)S(1)} %get-tuple-element.13.gt, bf16[256,2304]{1,0:T(8,128)(2,1)S(1)} %get-tuple-element.14.xs, ...), custom_call_target="tpu_custom_call" | custom-call | tf_op jit(solution)/shard_map/pallas_call | solution.py:663

commit v5 on v4

--- a/solution.py
+++ b/solution.py
@@ -91,8 +91,10 @@
 
 KC = 256
 DC = 128
-GC = 1024
+GC = 2048
+LC = 1024
 LAG0 = 8
+LATE = 3
 LAG1 = 7
 MESH = pl.DeviceIdType.MESH
 VMEM_LIMIT = 67043328
@@ -123,9 +125,9 @@
     n, J, res, shuf, mlp, enc, dec, bias, dbias,
     dg, xs, gt, parts,
     fx, e, enc_v, raw, xsend, xg, mlpx, msend, dsel, pre, pre_recv, feats,
-    nsend, nrecv, facc, osend, rr, rl, rc, rb, gacc, g_recv,
+    nsend, nrecv, facc, osend, rr, rl, rc, rb, gacc, g_send, g_recv,
     sem_l, sem_raw, x_s, x_r, y_s, m_s, m_r, p_s, p_r, f_s, f_r, n_s, n_r,
-    rs_s, rs_r, a_s, a_r, t_s, t_r, b_s, b_r, g_s, g_r, q_s, q_r,
+    rs_s, rs_r, a_s, a_r, t_s, t_r, b_s, b_r, g_s, g_r,
 ):
     z = lax.axis_index("feat")
     x = lax.axis_index("layer")
@@ -417,7 +419,13 @@
             pl.when(x == 1)(lambda: t_copy(j, z + h).start())
 
     def g_copy(k):
-        return remote(gacc.at[other_c, rows_of(k, GC)], g_recv.at[rows_of(k, GC)], g_s, g_r.at[k], row=other_c)
+        rows = rows_of(k, GC)
+        return remote(g_send.at[:, rows], g_recv.at[:, rows], g_s, g_r.at[k], row=other_c)
+
+    def send_grads(k):
+        rows = rows_of(k, GC)
+        g_send[:, rows, :] = gacc[:, rows, :].astype(BF)
+        g_copy(k).start()
 
     def grads(j):
         last = j == J - 1
@@ -427,7 +435,7 @@
             v = dot_last(dg[rows, wide(j)], e[j, 0].reshape(T, NC))
             gacc[0, rows, :] = gacc[0, rows, :] + v[:, :T2]
             gacc[1, rows, :] = gacc[1, rows, :] + v[:, T2:]
-            pl.when(last)(lambda: g_copy(k).start())
+            pl.when(last)(lambda: send_grads(k))
             return carry
 
         lax.fori_loop(0, F // GC, body, 0)
@@ -441,7 +449,7 @@
             v = dot_last(dg[rows, wide(j)], e[j, 0].reshape(T, NC)) + dot_last(dg[below, wide(j)], e[j, 1].reshape(T, NC))
             gacc[0, rows, :] = gacc[0, rows, :] + v[:, :T2]
             gacc[1, rows, :] = gacc[1, rows, :] + v[:, T2:]
-            pl.when(last)(lambda: g_copy(k).start())
+            pl.when(last)(lambda: send_grads(k))
             return carry
 
         lax.fori_loop(0, F // GC, body, 0)
@@ -486,12 +494,13 @@
         (0, None, front), (1, None, relay_near), (2, None, relay_far), (3, None, final), (3, None, early_b),
         (4, None, lambda j: hop(j, 1)), (5, None, lambda j: hop(j, 2)), (6, None, lambda j: hop(j, 3)), (6, None, late_b),
         (LAG1, 1, grads), (LAG1 + 1, 1, weights), (LAG0, 0, both_grads), (LAG0, 0, both_weights))
-    steps = J + max(LAG0, LAG1 + 1)
+    steps = J + max(LAG0, LAG1)
     share = pl.cdiv(nd, LAG0)
 
     def pipe(s, carry):
         for lag, side, act in stages:
-            live = jnp.logical_and(s >= lag, s < J + lag)
+            end = J - LATE if act in (weights, both_weights) else J
+            live = jnp.logical_and(s >= lag, s < end + lag)
             if side is not None:
                 live = jnp.logical_and(live, x == side)
             pl.when(live)(functools.partial(act, s - lag))
@@ -509,21 +518,38 @@
 
     lax.fori_loop(0, steps, pipe, 0)
 
-    def q_copy(k):
-        return remote(gt.at[c, rows_of(k, GC)], gt.at[c, rows_of(k, GC)], q_s, q_r.at[k], row=other_c)
+    spent = (J - LATE) * NC
+
+    def keep_fx(k, carry):
+        rows = rows_of(k, GC)
+        dg[rows, spent:spent + T] = fx[rows, :T]
+
+        @pl.when(x == 0)
+        def _():
+            dg[rows, spent + T:spent + 2 * T] = fx[rows, T:]
+
+        return carry
+
+    lax.fori_loop(0, 2 * F // GC, keep_fx, 0)
+    for h in range(LATE):
+        dg[2 * h * T:(2 * h + 1) * T, spent + 2 * T:spent + 2 * T + NC] = e[J - LATE + h, 0].reshape(T, NC)
+
+        @pl.when(x == 0)
+        def _():
+            dg[(2 * h + 1) * T:(2 * h + 2) * T, spent + 2 * T:spent + 2 * T + NC] = e[J - LATE + h, 1].reshape(T, NC)
 
     def mask_body(k, carry):
         g_copy(k).wait_recv()
         rows = rows_of(k, GC)
-        seen = jnp.concatenate([feats[k * (GC // KC) + i, mine, :] for i in range(GC // KC)], axis=1).T
-        v = (gacc[c, rows, :] + g_recv[rows, :]) * scale
-        gt[c, rows, :] = jnp.where(seen.astype(jnp.float32) > 0, v, 0.0).astype(BF)
-        q_copy(k).start()
+        for h in range(2):
+            seen = jnp.concatenate(
+                [feats[k * (GC // KC) + i, h * T2:(h + 1) * T2, :] for i in range(GC // KC)], axis=1).T
+            v = (g_send[h, rows, :].astype(jnp.float32) + g_recv[h, rows, :].astype(jnp.float32)) * scale
+            gt[h, rows, :] = jnp.where(seen.astype(jnp.float32) > 0, v, 0.0).astype(BF)
         return carry
 
     lax.fori_loop(0, F // GC, mask_body, 0)
     rb[x, c] = rc[c]
-
     theirs = pl.ds(pl.multiple_of(other_c * T2, T2), T2)
     remote(pre.at[:, theirs], pre_recv, p_s, p_r.at[0], row=other_c).wait_send()
     all_f.wait_send()
@@ -566,56 +592,89 @@
     for k in range(1, 4):
         b_copy(k, None).wait_send()
 
-    def last_body(k, carry):
-        q_copy(k).wait_recv()
-        return carry
-
-    lax.fori_loop(0, F // GC, last_body, 0)
-    sent(gacc.at[other_c], g_s, row=other_c)
-    sent(gt.at[c], q_s, row=other_c)
-
-
-def weight_kernel(dg, gt, xs, parts, enc_grad, dec_grad, bgrad, rebuilt, ebuf, bbuf, rbuf, dsem, esem, bsem, rsem):
+    sent(g_send, g_s, row=other_c)
+
+
+def weight_kernel(
+    dg, gt, xs, parts, enc_grad, dec_grad, bgrad, rebuilt,
+    late, ebuf, bbuf, rbuf, dsem, lsem, esem, bsem, rsem,
+):
     F, T2 = gt.shape[1:]
-    H = xs.shape[1]
+    T, H = xs.shape
+    NC = KC
     R2 = parts.shape[0]
-    nb = F // KC
+    nb, nl = F // KC, F // LC
+    x = lax.axis_index("layer")
+    scale = float(T) ** (-0.5)
+    done = H - LATE * NC
 
     def rows_of(i, size):
         return pl.ds(pl.multiple_of(i * size, size), size)
 
     def d_copy(i):
         rows = rows_of(i, 2 * KC)
-        return pltpu.make_async_copy(dg.at[rows], dec_grad.reshape(2 * F, H).at[rows], dsem.at[i])
+        return pltpu.make_async_copy(
+            dg.at[rows, pl.ds(0, done)], dec_grad.reshape(2 * F, H).at[rows, pl.ds(0, done)], dsem.at[i])
+
+    def l_copy(i):
+        rows = rows_of(i, 2 * LC)
+        return pltpu.make_async_copy(
+            late.at[rows], dec_grad.reshape(2 * F, H).at[rows, pl.ds(done, LATE * NC)], lsem.at[i])
 
     def e_copy(i):
-        rows = rows_of(i, KC)
-        return pltpu.make_async_copy(ebuf.at[rows], enc_grad.at[rows], esem.at[i])
+        slot = lax.rem(i, 4)
+        return pltpu.make_async_copy(ebuf.at[slot], enc_grad.at[rows_of(i, KC)], esem.at[slot])
 
     b_copy = pltpu.make_async_copy(bbuf, bgrad, bsem)
     r_copy = pltpu.make_async_copy(rbuf, rebuilt.reshape(R2, 2 * H), rsem)
     for i in range(nb):
         d_copy(i).start()
+
+    def late_block(i, carry):
+        rows = rows_of(i, 2 * LC)
+
+        def chunk(h, inner):
+            cols = rows_of(h, NC)
+
+            @pl.when(x == 0)
+            def _():
+                late[rows, cols] = (scale * mm(dg[rows, done:done + 2 * T], dg[rows_of(h, 2 * T), done + 2 * T:done + 2 * T + NC])).astype(BF)
+
+            @pl.when(x == 1)
+            def _():
+                late[rows, cols] = (scale * mm(dg[rows, done:done + T], dg[pl.ds(pl.multiple_of(2 * h * T, T), T), done + 2 * T:done + 2 * T + NC])).astype(BF)
+
+            return inner
+
+        lax.fori_loop(0, LATE, chunk, 0)
+        l_copy(i).start()
+        return carry
+
+    ones = jnp.ones((8, 2 * T2), BF)
+
+    def block(i, carry):
+        rows = rows_of(i, KC)
+        g = jnp.concatenate([gt[0, rows, :], gt[1, rows, :]], axis=1)
+        pl.when(i >= 4)(lambda: e_copy(i - 4).wait())
+        ebuf[lax.rem(i, 4)] = mm(g, xs[...]).astype(BF)
+        e_copy(i).start()
+        bbuf[:, rows] = dot_last(ones, g)[0:1]
+        return carry
+
+    lax.fori_loop(0, nl, late_block, 0)
     i = lax.broadcasted_iota(jnp.int32, (R2, R2), 0)
     j = lax.broadcasted_iota(jnp.int32, (R2, R2), 1)
     inter = (j == (i % 2) * (R2 // 2) + i // 2).astype(BF)
     rbuf[...] = mm(inter, parts[...]).astype(BF)
     r_copy.start()
-    ones = jnp.ones((8, 2 * T2), BF)
-
-    def block(i, carry):
-        rows = rows_of(i, KC)
-        g = jnp.concatenate([gt[0, rows, :], gt[1, rows, :]], axis=1)
-        ebuf[rows, :] = mm(g, xs[...]).astype(BF)
-        e_copy(i).start()
-        bbuf[:, rows] = dot_last(ones, g)[0:1]
-        return carry
-
     lax.fori_loop(0, nb, block, 0)
     b_copy.start()
     for i in range(nb):
         d_copy(i).wait()
+    for i in range(max(nb - 4, 0), nb):
         e_copy(i).wait()
+    for i in range(nl):
+        l_copy(i).wait()
     r_copy.wait()
     b_copy.wait()
 
@@ -644,18 +703,18 @@
         in_specs=[vm, vm, vm, hbm, hbm, vm, vm],
         out_specs=(vm,) * 4,
         scratch_shapes=[
-            vmem((2 * F, 2 * T), BF), vmem((J, 2, n, CR, NC), BF), vmem((F, H), BF), vmem((4, 2 * DC, H), BF),
+            vmem((2 * F, 2 * T), BF), vmem((J, 2, n, CR, NC), BF), vmem((F, H), BF), vmem((3, 2 * DC, H), BF),
             vmem((2, Q, R, HX), BF), vmem((n, 2, Q, R, HX), BF),
             vmem((2, R, H), BF), vmem((R, H), BF), vmem((1, H), f32),
             vmem((nk, T, KC), f32), vmem((nk, T2, KC), f32), vmem((nk, T, KC), BF),
             vmem((J, T, NC), BF), vmem((J, T, NC), BF), vmem((J, n, CR, NC), f32),
             vmem((J, n, CR, NC), BF), vmem((J, n, CR, NC), BF), vmem((J, n, CR, NC), BF),
             vmem((2, J, R, NC), BF), vmem((2, 2, J, R, NC), BF),
-            vmem((2, F, T2), f32), vmem((F, T2), f32),
+            vmem((2, F, T2), f32), vmem((2, F, T2), BF), vmem((2, F, T2), BF),
             dma, dma((4,)), dma((n, 2)), dma((n, 2, Q)), dma((2,)), dma, dma,
             dma, dma((nk,)), dma, dma, dma, dma((J,)),
             dma((2,)), dma((J, 2, 2)), dma((2,)), dma((J, n)), dma, dma((J,)),
-            dma((4,)), dma((4,)), dma, dma((F // GC,)), dma, dma((F // GC,)),
+            dma((4,)), dma((4,)), dma, dma((F // GC,)),
         ],
         compiler_params=pltpu.CompilerParams(
             collective_id=0, has_side_effects=True, vmem_limit_bytes=VMEM_LIMIT - held),
@@ -667,8 +726,9 @@
         in_specs=[vm] * 4,
         out_specs=(hbm,) * 4,
         scratch_shapes=[
-            vmem((F, H), BF), vmem((1, F), f32), vmem((2 * R, 2 * H), BF), dma((nk,)), dma((nk,)), dma, dma],
-        compiler_params=pltpu.CompilerParams(vmem_limit_bytes=VMEM_LIMIT // 3),
+            vmem((2 * F, LATE * NC), BF), vmem((4, KC, H), BF), vmem((1, F), f32), vmem((2 * R, 2 * H), BF),
+            dma((nk,)), dma((F // LC,)), dma((4,)), dma, dma],
+        compiler_params=pltpu.CompilerParams(vmem_limit_bytes=VMEM_LIMIT // 4),
     )(dg, gt, xs, parts)
     return rebuilt, enc_grad[None], dec_grad[None], bgrad
 
@@ -679,7 +739,8 @@
     fits = (
         lax.axis_size("layer") == LAYERS == 2 and lax.axis_size("row") == 2
         and lax.axis_size("feat") == 4 and rows % 16 == 0
-        and width % KC == 0 and width // KC >= 3 and enc_weight.shape[1] % GC == 0)
+        and width % KC == 0 and width // KC > LATE
+        and rows * 2 * lax.axis_size("feat") == KC and enc_weight.shape[1] % GC == 0)
     return fused(*args) if fits else on_device(*args)
 
 

time: 103 us -> 99.7 us (0.968)
  Pallas kernels: 102 us -> 98.3 us
    pallas_call x1, Pallas kernels: 92.3 us -> 88.1 us  [fused(): pl.pallas_call(functools.partial(step_kernel, n, J), out_shape=tuple((vme...]
where the time goes in v5:
time: 99.7 us; the launch traced here: 98.9 us
  Pallas kernels  98.3 us (99%)
    pallas_call x1, Pallas kernels, fused(): pl.pallas_call(functools.partial(step_kernel, n, J), out_shape=tuple((vme...  88.1 us
    pallas_call x1, Pallas kernels, fused(): pl.pallas_call(weight_kernel, out_shape=(shape((F, H), BF), shape((F, 2,...  10.1 us

profile of v5, /device:TPU:0, one launch (start us, length us, event | category | flops | bytes accessed | tf_op | source)
XLA Modules:
  0.0 98.9 jit_solution(4745329734402361283)
XLA Ops:
  0.6 88.1 %shard_map.102 = (bf16[4096,2304]{1,0:T(8,128)(2,1)S(1)}, bf16[256,2304]{1,0:T(8,128)(2,1)S(1)}, bf16[2,2048,128]{2,1,0:T(8,128)(2,1)S(1)}, bf16[64,4608]{1,0:T(8,128)(2,1)S(1)}) custom-call(bf16[32,2,4608]{2,1,0:T(2,128)(2,1)} %res.1, s32[1,256]{1,0:T(1,128)} %bitcast.7, bf16[32,2,4608]{2,1,0:T(2,128)(2,1)} %mlp.1, bf16[2048,2304]{1,0:T(8,128)(2,1)} %bitcast.6, ...), custom_call_target="tpu_custom_call" | custom-call | tf_op jit(solution)/shard_map/pallas_call | solution.py:700
  88.8 10.1 %shard_map.103 = (bf16[2048,2304]{1,0:T(8,128)(2,1)}, bf16[2048,2,2304]{2,1,0:T(2,128)(2,1)}, f32[1,2048]{1,0:T(1,128)}, bf16[32,2,4608]{2,1,0:T(2,128)(2,1)}) custom-call(bf16[4096,2304]{1,0:T(8,128)(2,1)S(1)} %get-tuple-element.12.dg, bf16[2,2048,128]{2,1,0:T(8,128)(2,1)S(1)} %get-tuple-element.13.gt, bf16[256,2304]{1,0:T(8,128)(2,1)S(1)} %get-tuple-element.14.xs, ...), custom_call_target="tpu_custom_call" | custom-call | tf_op jit(solution)/shard_map/pallas_call | solution.py:722

commit v6 on v5

--- a/solution.py
+++ b/solution.py
@@ -93,6 +93,7 @@
 DC = 128
 GC = 2048
 LC = 1024
+GB = 512
 LAG0 = 8
 LATE = 3
 LAG1 = 7
@@ -123,9 +124,9 @@
 
 def step_kernel(
     n, J, res, shuf, mlp, enc, dec, bias, dbias,
-    dg, xs, gt, parts,
+    dg, xs, gt, rb,
     fx, e, enc_v, raw, xsend, xg, mlpx, msend, dsel, pre, pre_recv, feats,
-    nsend, nrecv, facc, osend, rr, rl, rc, rb, gacc, g_send, g_recv,
+    nsend, nrecv, facc, osend, rr, rl, rc, gacc, g_send, g_recv,
     sem_l, sem_raw, x_s, x_r, y_s, m_s, m_r, p_s, p_r, f_s, f_r, n_s, n_r,
     rs_s, rs_r, a_s, a_r, t_s, t_r, b_s, b_r, g_s, g_r,
 ):
@@ -246,6 +247,14 @@
     lax.fori_loop(0, nd // 2, split_body, 0)
     pass_on(0)
     lax.fori_loop(nd // 2, nd, split_body, 0)
+    def rows_of(k, size, base=0):
+        return pl.ds(pl.multiple_of(base + k * size, KC), size)
+
+    def zero_body(k, carry):
+        gacc[:, rows_of(k, KC), :] = jnp.zeros((2, KC, T2), jnp.float32)
+        return carry
+
+    lax.fori_loop(0, nk, zero_body, 0)
     enc_copy.wait()
     per = 2 if nk % 2 == 0 else 1
     for q in range(Q):
@@ -280,14 +289,6 @@
 
     lax.fori_loop(0, nk, feat_body, 0)
 
-    def rows_of(k, size, base=0):
-        return pl.ds(pl.multiple_of(base + k * size, KC), size)
-
-    def zero_body(k, carry):
-        gacc[:, rows_of(k, KC), :] = jnp.zeros((2, KC, T2), jnp.float32)
-        return carry
-
-    lax.fori_loop(0, nk, zero_body, 0)
     all_f = remote(feats.at[:, mine], feats.at[:, mine], f_s, f_r, row=other_c)
     all_f.wait_recv()
     m_copy.wait_recv()
@@ -419,40 +420,40 @@
             pl.when(x == 1)(lambda: t_copy(j, z + h).start())
 
     def g_copy(k):
-        rows = rows_of(k, GC)
+        rows = rows_of(k, GB)
         return remote(g_send.at[:, rows], g_recv.at[:, rows], g_s, g_r.at[k], row=other_c)
 
-    def send_grads(k):
-        rows = rows_of(k, GC)
-        g_send[:, rows, :] = gacc[:, rows, :].astype(BF)
-        g_copy(k).start()
+    def add_grads(j, k, size, both):
+        rows = rows_of(k, size)
+        v = dot_last(dg[rows, wide(j)], e[j, 0].reshape(T, NC))
+        if both:
+            v = v + dot_last(dg[rows_of(k, size, F), wide(j)], e[j, 1].reshape(T, NC))
+        gacc[0, rows, :] = gacc[0, rows, :] + v[:, :T2]
+        gacc[1, rows, :] = gacc[1, rows, :] + v[:, T2:]
+
+    def sum_grads(j, both):
+        @pl.when(j < J - 1)
+        def _():
+            for k in range(F // GC):
+                add_grads(j, k, GC, both)
+
+        @pl.when(j == J - 1)
+        def _():
+            def body(k, carry):
+                add_grads(j, k, GB, both)
+                rows = rows_of(k, GB)
+                g_send[:, rows, :] = gacc[:, rows, :].astype(BF)
+                g_copy(k).start()
+                return carry
+
+            lax.fori_loop(0, F // GB, body, 0)
 
     def grads(j):
-        last = j == J - 1
-
-        def body(k, carry):
-            rows = rows_of(k, GC)
-            v = dot_last(dg[rows, wide(j)], e[j, 0].reshape(T, NC))
-            gacc[0, rows, :] = gacc[0, rows, :] + v[:, :T2]
-            gacc[1, rows, :] = gacc[1, rows, :] + v[:, T2:]
-            pl.when(last)(lambda: send_grads(k))
-            return carry
-
-        lax.fori_loop(0, F // GC, body, 0)
+        sum_grads(j, False)
 
     def both_grads(j):
-        last = j == J - 1
         remote(e.at[j, 0], e.at[j, 1], t_s, t_r.at[j], layer=other_x).wait_recv()
-
-        def body(k, carry):
-            rows, below = rows_of(k, GC), rows_of(k, GC, F)
-            v = dot_last(dg[rows, wide(j)], e[j, 0].reshape(T, NC)) + dot_last(dg[below, wide(j)], e[j, 1].reshape(T, NC))
-            gacc[0, rows, :] = gacc[0, rows, :] + v[:, :T2]
-            gacc[1, rows, :] = gacc[1, rows, :] + v[:, T2:]
-            pl.when(last)(lambda: send_grads(k))
-            return carry
-
-        lax.fori_loop(0, F // GC, body, 0)
+        sum_grads(j, True)
 
     def weights(j):
         def body(k, carry):
@@ -540,15 +541,15 @@
 
     def mask_body(k, carry):
         g_copy(k).wait_recv()
-        rows = rows_of(k, GC)
+        rows = rows_of(k, GB)
         for h in range(2):
             seen = jnp.concatenate(
-                [feats[k * (GC // KC) + i, h * T2:(h + 1) * T2, :] for i in range(GC // KC)], axis=1).T
+                [feats[k * (GB // KC) + i, h * T2:(h + 1) * T2, :] for i in range(GB // KC)], axis=1).T
             v = (g_send[h, rows, :].astype(jnp.float32) + g_recv[h, rows, :].astype(jnp.float32)) * scale
             gt[h, rows, :] = jnp.where(seen.astype(jnp.float32) > 0, v, 0.0).astype(BF)
         return carry
 
-    lax.fori_loop(0, F // GC, mask_body, 0)
+    lax.fori_loop(0, F // GB, mask_body, 0)
     rb[x, c] = rc[c]
     theirs = pl.ds(pl.multiple_of(other_c * T2, T2), T2)
     remote(pre.at[:, theirs], pre_recv, p_s, p_r.at[0], row=other_c).wait_send()
@@ -585,10 +586,6 @@
     pl.when(x == 1)(lambda: sent(e.at[:, 0], t_s, layer=other_x))
     for k in range(1, 4):
         b_copy(k, None).wait_recv()
-    for h in range(2):
-        for j in range(J):
-            lo = h * H + j * NC
-            parts[:, lo:lo + NC] = rb[:, h, j].reshape(2 * R, NC)
     for k in range(1, 4):
         b_copy(k, None).wait_send()
 
@@ -596,8 +593,8 @@
 
 
 def weight_kernel(
-    dg, gt, xs, parts, enc_grad, dec_grad, bgrad, rebuilt,
-    late, ebuf, bbuf, rbuf, dsem, lsem, esem, bsem, rsem,
+    dg, gt, xs, rb, enc_grad, dec_grad, bgrad, rebuilt,
+    parts, late, ebuf, bbuf, rbuf, dsem, lsem, esem, bsem, rsem,
 ):
     F, T2 = gt.shape[1:]
     T, H = xs.shape
@@ -662,6 +659,10 @@
         return carry
 
     lax.fori_loop(0, nl, late_block, 0)
+    for h in range(2):
+        for j in range(rb.shape[2]):
+            lo = h * H + j * NC
+            parts[:, lo:lo + NC] = rb[:, h, j].reshape(R2, NC)
     i = lax.broadcasted_iota(jnp.int32, (R2, R2), 0)
     j = lax.broadcasted_iota(jnp.int32, (R2, R2), 1)
     inter = (j == (i % 2) * (R2 // 2) + i // 2).astype(BF)
@@ -695,9 +696,9 @@
     dma = pltpu.SemaphoreType.DMA
     vmem = pltpu.VMEM
     shape = jax.ShapeDtypeStruct
-    outs = ((2 * F, H), (T, H), (2, F, T2), (2 * R, 2 * H))
+    outs = ((2 * F, H), (T, H), (2, F, T2), (2, 2, J, R, NC))
     held = sum(2 * math.prod(a) for a in outs)
-    dg, xs, gt, parts = pl.pallas_call(
+    dg, xs, gt, rb = pl.pallas_call(
         functools.partial(step_kernel, n, J),
         out_shape=tuple(vmem(a, BF) for a in outs),
         in_specs=[vm, vm, vm, hbm, hbm, vm, vm],
@@ -709,12 +710,12 @@
             vmem((nk, T, KC), f32), vmem((nk, T2, KC), f32), vmem((nk, T, KC), BF),
             vmem((J, T, NC), BF), vmem((J, T, NC), BF), vmem((J, n, CR, NC), f32),
             vmem((J, n, CR, NC), BF), vmem((J, n, CR, NC), BF), vmem((J, n, CR, NC), BF),
-            vmem((2, J, R, NC), BF), vmem((2, 2, J, R, NC), BF),
+            vmem((2, J, R, NC), BF),
             vmem((2, F, T2), f32), vmem((2, F, T2), BF), vmem((2, F, T2), BF),
             dma, dma((4,)), dma((n, 2)), dma((n, 2, Q)), dma((2,)), dma, dma,
             dma, dma((nk,)), dma, dma, dma, dma((J,)),
             dma((2,)), dma((J, 2, 2)), dma((2,)), dma((J, n)), dma, dma((J,)),
-            dma((4,)), dma((4,)), dma, dma((F // GC,)),
+            dma((4,)), dma((4,)), dma, dma((F // GB,)),
         ],
         compiler_params=pltpu.CompilerParams(
             collective_id=0, has_side_effects=True, vmem_limit_bytes=VMEM_LIMIT - held),
@@ -726,10 +727,10 @@
         in_specs=[vm] * 4,
         out_specs=(hbm,) * 4,
         scratch_shapes=[
-            vmem((2 * F, LATE * NC), BF), vmem((4, KC, H), BF), vmem((1, F), f32), vmem((2 * R, 2 * H), BF),
+            vmem((2 * R, 2 * H), BF), vmem((2 * F, LATE * NC), BF), vmem((4, KC, H), BF), vmem((1, F), f32), vmem((2 * R, 2 * H), BF),
             dma((nk,)), dma((F // LC,)), dma((4,)), dma, dma],
         compiler_params=pltpu.CompilerParams(vmem_limit_bytes=VMEM_LIMIT // 4),
-    )(dg, gt, xs, parts)
+    )(dg, gt, xs, rb)
     return rebuilt, enc_grad[None], dec_grad[None], bgrad
 
 

time: 99.7 us -> 98.8 us (level)
  no operation moved by 1% of the time
where the time goes in v6:
time: 98.8 us; the launch traced here: 98.4 us
  Pallas kernels  97.8 us (99%)
    pallas_call x1, Pallas kernels, fused(): pl.pallas_call(functools.partial(step_kernel, n, J), out_shape=tuple((vme...  87.7 us
    pallas_call x1, Pallas kernels, fused(): pl.pallas_call(weight_kernel, out_shape=(shape((F, H), BF), shape((F, 2,...  10.1 us

profile of v6, /device:TPU:0, one launch (start us, length us, event | category | flops | bytes accessed | tf_op | source)
XLA Modules:
  0.0 98.4 jit_solution(16565048583964214362)
XLA Ops:
  0.6 87.7 %shard_map.102 = (bf16[4096,2304]{1,0:T(8,128)(2,1)S(1)}, bf16[256,2304]{1,0:T(8,128)(2,1)S(1)}, bf16[2,2048,128]{2,1,0:T(8,128)(2,1)S(1)}, bf16[2,2,9,32,256]{4,3,2,1,0:T(8,128)(2,1)S(1)}) custom-call(bf16[32,2,4608]{2,1,0:T(2,128)(2,1)} %res.1, s32[1,256]{1,0:T(1,128)} %bitcast.7, bf16[32,2,4608]{2,1,0:T(2,128)(2,1)} %mlp.1, bf16[2048,2304]{1,0:T(8,128)(2,1)} %bitcast.6, ...), custom_call_target="tpu_custom_call" | custom-call | tf_op jit(solution)/shard_map/pallas_call | solution.py:701
  88.3 10.1 %shard_map.103 = (bf16[2048,2304]{1,0:T(8,128)(2,1)}, bf16[2048,2,2304]{2,1,0:T(2,128)(2,1)}, f32[1,2048]{1,0:T(1,128)}, bf16[32,2,4608]{2,1,0:T(2,128)(2,1)}) custom-call(bf16[4096,2304]{1,0:T(8,128)(2,1)S(1)} %get-tuple-element.12.dg, bf16[2,2048,128]{2,1,0:T(8,128)(2,1)S(1)} %get-tuple-element.13.gt, bf16[256,2304]{1,0:T(8,128)(2,1)S(1)} %get-tuple-element.14.xs, ...), custom_call_target="tpu_custom_call" | custom-call | tf_op jit(solution)/shard_map/pallas_call | solution.py:723

commit v7 on v6

--- a/solution.py
+++ b/solution.py
@@ -92,7 +92,7 @@
 KC = 256
 DC = 128
 GC = 2048
-LC = 1024
+LC = 2048
 GB = 512
 LAG0 = 8
 LATE = 3
@@ -729,7 +729,7 @@
         scratch_shapes=[
             vmem((2 * R, 2 * H), BF), vmem((2 * F, LATE * NC), BF), vmem((4, KC, H), BF), vmem((1, F), f32), vmem((2 * R, 2 * H), BF),
             dma((nk,)), dma((F // LC,)), dma((4,)), dma, dma],
-        compiler_params=pltpu.CompilerParams(vmem_limit_bytes=VMEM_LIMIT // 4),
+        compiler_params=pltpu.CompilerParams(vmem_limit_bytes=VMEM_LIMIT // 3),
     )(dg, gt, xs, rb)
     return rebuilt, enc_grad[None], dec_grad[None], bgrad
 

time: 98.8 us -> 98.8 us (level)
  no operation moved by 1% of the time
where the time goes in v7:
time: 98.8 us; the launch traced here: 98.4 us
  Pallas kernels  97.8 us (99%)
    pallas_call x1, Pallas kernels, fused(): pl.pallas_call(functools.partial(step_kernel, n, J), out_shape=tuple((vme...  87.7 us
    pallas_call x1, Pallas kernels, fused(): pl.pallas_call(weight_kernel, out_shape=(shape((F, H), BF), shape((F, 2,...  10.1 us

profile of v7, /device:TPU:0, one launch (start us, length us, event | category | flops | bytes accessed | tf_op | source)
XLA Modules:
  0.0 98.4 jit_solution(7200726872339182753)
XLA Ops:
  0.6 87.7 %shard_map.102 = (bf16[4096,2304]{1,0:T(8,128)(2,1)S(1)}, bf16[256,2304]{1,0:T(8,128)(2,1)S(1)}, bf16[2,2048,128]{2,1,0:T(8,128)(2,1)S(1)}, bf16[2,2,9,32,256]{4,3,2,1,0:T(8,128)(2,1)S(1)}) custom-call(bf16[32,2,4608]{2,1,0:T(2,128)(2,1)} %res.1, s32[1,256]{1,0:T(1,128)} %bitcast.7, bf16[32,2,4608]{2,1,0:T(2,128)(2,1)} %mlp.1, bf16[2048,2304]{1,0:T(8,128)(2,1)} %bitcast.6, ...), custom_call_target="tpu_custom_call" | custom-call | tf_op jit(solution)/shard_map/pallas_call | solution.py:701
  88.3 10.1 %shard_map.103 = (bf16[2048,2304]{1,0:T(8,128)(2,1)}, bf16[2048,2,2304]{2,1,0:T(2,128)(2,1)}, f32[1,2048]{1,0:T(1,128)}, bf16[32,2,4608]{2,1,0:T(2,128)(2,1)}) custom-call(bf16[4096,2304]{1,0:T(8,128)(2,1)S(1)} %get-tuple-element.12.dg, bf16[2,2048,128]{2,1,0:T(8,128)(2,1)S(1)} %get-tuple-element.13.gt, bf16[256,2304]{1,0:T(8,128)(2,1)S(1)} %get-tuple-element.14.xs, ...), custom_call_target="tpu_custom_call" | custom-call | tf_op jit(solution)/shard_map/pallas_call | solution.py:723
